TPU v7x, 128 devices: a whole 4x4x4 slice. The times are simulated.
128 devices in a mesh: region: 32 (over z, x, core), obs: 4 (over y).
Axes of the slice: x: 4, y: 4, z: 4, core: 2. Of those that a mesh axis runs over, the one named last changes fastest.
Arguments:
- pattern: int32 [1048576], P(('region', 'obs')), may hold values from 0 to 511
- amplitude: float32 [5, 1048576], P(None, ('region', 'obs')), may hold values from 0.5 to 1.5
- basis_table: bfloat16 [5, 512, 128], replicated, may hold values from -2 to 2, as said below
- fields: bfloat16 [64, 1048576], P(None, ('region', 'obs')), may hold values from -24 to 24
- prior_precision: float32 [5, 128], replicated, may hold values from 16 to 512
Outputs:
- fitted: float32 [64, 1048576], P(None, ('region', 'obs'))
Inputs may be any that keep to these rules, and one draw needn't show every extreme that they name: `basis_table`: basis rows of different tiers for one pattern are correlated.
All inputs are finite; a program needn't handle non-finite values.
Results may differ from a plain program's by a relative error of at most 0.0062.
Values sent between devices are 32-bit elements; how exact they have to be, the bound alone decides.
A program may use at most 64 MiB of HBM per device.

v0:
```python
import functools

import jax
import jax.numpy as jnp
from jax import lax
from jax.experimental import pallas as pl
from jax.experimental.pallas import tpu as pltpu
from jax.sharding import PartitionSpec as P

f32 = jnp.float32
bf16 = jnp.bfloat16
highest = lax.Precision.HIGHEST
PANEL = 16
PAIR_ROW = {(0, 3): 5, (1, 4): 6, (0, 4): 7, (0, 1): 8, (1, 2): 9, (2, 3): 10, (3, 4): 11,
            (0, 2): 12, (1, 3): 13, (2, 4): 14, (0, 0): 0, (1, 1): 1, (2, 2): 2, (3, 3): 3, (4, 4): 4}


def iota(shape, axis):
    return lax.broadcasted_iota(jnp.int32, shape, axis)


def swapped(value, axis, stride):
    mask = 2**stride
    pairs = [(source, source ^ mask) for source in range(lax.axis_size(axis))]
    return lax.ppermute(value, axis, pairs)


def amplitude_products(amp):
    n = amp.shape[1]
    a8 = jnp.concatenate([amp, jnp.zeros((3, n), f32)], axis=0)
    sub = iota((8, n), 0)
    up = lambda s: pltpu.roll(a8, s, 0)
    l0 = jnp.where(sub < 5, a8, jnp.where(sub < 7, up(5), up(7)))
    r0 = jnp.where(sub < 5, a8, jnp.where(sub < 7, up(2), up(3)))
    l1 = jnp.where(sub < 4, a8, jnp.where(sub < 7, up(4), 0.0))
    r1 = jnp.where(sub < 4, up(7), up(2))
    return jnp.concatenate([l0 * r0, l1 * r1], axis=0)


def one_hot(pattern_ref, first_row, rows, patterns):
    parts = []
    ids = iota((patterns, 128), 0)
    for r in range(rows):
        row = pattern_ref[pl.ds(first_row + r, 1), :]
        parts.append((jnp.broadcast_to(row, (patterns, 128)) == ids).astype(f32).astype(bf16))
    return jnp.concatenate(parts, axis=1)


def stats_kernel(pattern_ref, amp_ref, table_ref, fields_ref, w_ref, c_ref, acc_ref, *, chunk):
    tiers, patterns, knots = table_ref.shape
    obs = amp_ref.shape[1]
    nf = fields_ref.shape[0]
    acc_ref[...] = jnp.zeros_like(acc_ref)

    def step(i, carry):
        off = pl.multiple_of(i * chunk, chunk)
        amp = amp_ref[:, pl.ds(off, chunk)]
        fields = fields_ref[:, pl.ds(off, chunk)].astype(f32)
        prod = amplitude_products(amp)
        hi = prod.astype(bf16)
        lo = (prod - hi.astype(f32)).astype(bf16)
        rows = [(fields * amp[t:t + 1, :]).astype(bf16) for t in range(tiers)]
        lhs = jnp.concatenate(rows + [hi, lo], axis=0)
        hot = one_hot(pattern_ref, i * (chunk // 128), chunk // 128, patterns)
        acc_ref[...] += lax.dot_general(lhs, hot, (((1,), (1,)), ((), ())), preferred_element_type=f32)
        return carry

    lax.fori_loop(0, obs // chunk, step, 0)
    base = tiers * nf
    w_ref[...] = acc_ref[base:base + 16, :] + acc_ref[base + 16:base + 32, :]
    for t in range(tiers):
        v = acc_ref[t * nf:(t + 1) * nf, :]
        hi = v.astype(bf16)
        lo = (v - hi.astype(f32)).astype(bf16)
        both = jnp.dot(jnp.concatenate([hi, lo], axis=0), table_ref[t], preferred_element_type=f32)
        c_ref[:, t * knots:(t + 1) * knots] = both[:nf] + both[nf:]


def fit_kernel(pattern_ref, amp_ref, f_ref, out_ref):
    tiers = amp_ref.shape[0]
    nf, chunk = out_ref.shape
    hot = one_hot(pattern_ref, 0, chunk // 128, f_ref.shape[1])
    part = jnp.dot(f_ref[...], hot, preferred_element_type=f32)
    total = part[:nf] * amp_ref[0:1, :]
    for t in range(1, tiers):
        total = total + part[t * nf:(t + 1) * nf] * amp_ref[t:t + 1, :]
    out_ref[...] = total


def inverse_factor_kernel(a_ref, o_ref, m_ref, q_ref):
    n = a_ref.shape[0]
    sub, lane, lane2 = iota((PANEL, n), 0), iota((PANEL, n), 1), iota((n, n), 1)
    m_ref[...] = a_ref[...]
    q_ref[...] = jnp.zeros((n, n), f32)

    def body(b, carry):
        off = pl.multiple_of(b * PANEL, PANEL)
        whole = m_ref[...]
        rows = m_ref[pl.ds(off, PANEL), :]
        cols = [
            jnp.take_along_axis(rows, jnp.zeros((PANEL, n), jnp.int32) + (off + l), axis=1)
            for l in range(PANEL)
        ]
        inside = (lane >= off) & (lane < off + PANEL)
        x = jnp.where(lane - off == sub, 1.0, jnp.where(inside, 0.0, rows))
        outs = x
        for j in range(PANEL):
            pick = lambda v: jnp.broadcast_to(v[j:j + 1, :], (PANEL, n))
            pivot = pick(cols[j])
            inv = 1.0 / pivot
            xj = pick(x)
            outs = jnp.where(sub == j, xj * lax.rsqrt(pivot), outs)
            mult = jnp.where(sub == j, inv, -cols[j] * inv)
            for l in range(j + 1, PANEL):
                cols[l] = jnp.where(sub == j, 0.0, cols[l]) + mult * pick(cols[l])
            x = jnp.where(sub == j, 0.0, x) + mult * xj
        o_ref[pl.ds(off, PANEL), :] = jnp.where(lane - off <= sub, outs, 0.0)
        q_ref[pl.ds(off, PANEL), :] = x
        update = jnp.dot(whole, q_ref[...], precision=highest, preferred_element_type=f32)
        q_ref[pl.ds(off, PANEL), :] = jnp.zeros((PANEL, n), f32)
        m_ref[...] = jnp.where((lane2 >= off) & (lane2 < off + PANEL), 0.0, whole) - update
        return carry

    lax.fori_loop(0, n // PANEL, body, 0)


def inverse_factor(a):
    n = a.shape[0]
    return pl.pallas_call(
        inverse_factor_kernel,
        out_shape=jax.ShapeDtypeStruct((n, n), f32),
        scratch_shapes=[pltpu.VMEM((n, n), f32)] * 2,
    )(a)


def add_prior(matrix, prior_precision, tier_index):
    offset = tier_index * prior_precision.shape[1]
    return matrix.at[offset:, offset:].add(jnp.diag(prior_precision[tier_index]))


def dot(a, b):
    return jnp.dot(a, b, precision=highest)


def eliminate(matrix, rhs_rows, tier_index, knot_count):
    offset = tier_index * knot_count
    factor = inverse_factor(matrix[offset:, offset:])
    whiten = dot(factor, rhs_rows[:, offset:].T)
    coupling = dot(factor, matrix[offset:, :offset])
    schur_part = matrix[:offset, :offset] - dot(coupling.T, coupling)
    reduced = rhs_rows[:, :offset] - dot(whiten.T, coupling)
    return (factor, coupling, whiten, schur_part, reduced)


def shards(pattern, amplitude, basis_table, fields, prior_precision):
    tiers, patterns, knots = basis_table.shape
    ancestors = tiers - 1
    obs = pattern.shape[0]
    nf = fields.shape[0]
    pattern2 = pattern.reshape(obs // 128, 128)
    w, c = pl.pallas_call(
        functools.partial(stats_kernel, chunk=1024),
        out_shape=(jax.ShapeDtypeStruct((16, patterns), f32), jax.ShapeDtypeStruct((nf, tiers * knots), f32)),
        scratch_shapes=[pltpu.VMEM((tiers * nf + 32, patterns), f32)],
    )(pattern2, amplitude, basis_table, fields)
    w, rhs_rows = lax.psum((w, c), "obs")
    table = basis_table.astype(f32)
    blocks = [[None] * tiers for _ in range(tiers)]
    for s in range(tiers):
        for t in range(s, tiers):
            blk = jnp.einsum("pk,pl->kl", table[t] * w[PAIR_ROW[(s, t)]][:, None], table[s], precision=highest)
            blocks[t][s] = blk
            blocks[s][t] = blk.T if t > s else blk
    matrix = jnp.concatenate([jnp.concatenate(row, axis=1) for row in blocks], axis=0)
    matrix = add_prior(matrix, prior_precision, ancestors)
    region_bits = lax.axis_size("region").bit_length() - 1
    stored = {}
    for tier_index in range(ancestors, 0, -1):
        factor, coupling, whiten, schur_part, reduced = eliminate(matrix, rhs_rows, tier_index, knots)
        stored[tier_index] = (factor, coupling, whiten)
        bits = [ancestors - tier_index] if tier_index > 1 else range(ancestors - 1, region_bits)
        for bit in bits:
            other_mat, other_rhs = swapped((schur_part, reduced), "region", bit)
            schur_part = schur_part + other_mat
            reduced = reduced + other_rhs
        matrix = add_prior(schur_part, prior_precision, tier_index - 1)
        rhs_rows = reduced
    root = inverse_factor(matrix)
    path = dot(root.T, dot(root, rhs_rows.T))
    for tier_index in range(1, tiers):
        factor, coupling, whiten = stored[tier_index]
        path = jnp.concatenate([path, dot(factor.T, whiten - dot(coupling, path))], axis=0)
    per_pattern = jnp.concatenate(
        [dot(path[t * knots:(t + 1) * knots].T, table[t].T) for t in range(tiers)], axis=0
    ).astype(bf16)
    chunk = min(1024, obs)
    return pl.pallas_call(
        fit_kernel,
        grid=(obs // chunk,),
        in_specs=[
            pl.BlockSpec((chunk // 128, 128), lambda i: (i, 0)),
            pl.BlockSpec((tiers, chunk), lambda i: (0, i)),
            pl.BlockSpec((tiers * nf, patterns), lambda i: (0, 0)),
        ],
        out_specs=pl.BlockSpec((nf, chunk), lambda i: (0, i)),
        out_shape=jax.ShapeDtypeStruct((nf, obs), f32),
    )(pattern2, amplitude, per_pattern)


def solution(mesh):
    return jax.shard_map(
        shards,
        mesh=mesh,
        in_specs=(
            P(("region", "obs")),
            P(None, ("region", "obs")),
            P(),
            P(None, ("region", "obs")),
            P(),
        ),
        out_specs=P(None, ("region", "obs")),
        check_vma=False,
    )
```

profile of v0, /device:TPU:0, one launch (start us, length us, event | category | flops | bytes accessed | tf_op | source)
XLA Modules:
  0.0 198.7 jit_solution(3345631362731861452)
XLA Ops:
  6.5 1.2 convert_element_type.4
  7.7 7.2 %shard_map.60 = (f32[16,512]{1,0:T(8,128)}, f32[64,640]{1,0:T(8,128)}) custom-call(s32[64,128]{1,0:T(8,128)} %bitcast.205, f32[5,8192]{1,0:T(8,128)} %amp_ref.3, bf16[5,512,128]{2,1,0:T(8,128)(2,1)} %table_ref.1, bf16[64,8192]{1,0:T(8,128)(2,1)} %fields_ref.1), custom_call_target="tpu_custom_call" | custom-call | tf_op jit(solution)/shard_map/pallas_call | solution.py:161
  15.0 18.0 %psum.14 = f32[16,512]{1,0:T(8,128)S(1)} all-reduce(f32[16,512]{1,0:T(8,128)} %get-tuple-element.75), channel_id=1, replica_groups=mesh['region'=32,'obs'=4] {'obs'}, use_global_device_ids=true, to_apply=%region_0.0 | all-reduce | flops 8192 | bytes 65536 | tf_op jit(solution)/shard_map/psum | solution.py:166
  33.1 1.1 constant_dynamic-update-slice_fusion.2
  36.0 1.1 constant_dynamic-update-slice_fusion.5
  42.6 1.1 convolution_add_fusion.a_ref
  43.8 4.9 %shard_map.61 = f32[128,128]{1,0:T(8,128)} custom-call(f32[128,128]{1,0:T(8,128)} %convolution_add_fusion.a_ref), custom_call_target="tpu_custom_call" | custom-call | tf_op jit(solution)/shard_map/pallas_call | solution.py:129
  51.1 1.2 fusion.7
  53.5 1.6 copy.7
  55.1 1.6 copy.8
  62.1 42.5 %all-reduce.2.cloned.1.call-done = f32[64,640]{1,0:T(8,128)} async-done(((f32[64,640]{1,0:T(8,128)}), f32[64,640]{1,0:T(8,128)}) %all-reduce.2.cloned.1.call-update) | async-done | bytes 163856 | tf_op jit(solution)/shard_map/psum | solution.py:166
  105.6 1.2 convolution_subtract_fusion.1
  107.0 1.4 add.72
  109.2 4.9 %shard_map.62 = f32[128,128]{1,0:T(8,128)} custom-call(f32[128,128]{1,0:T(8,128)} %slice_add_fusion.2.a_ref), custom_call_target="tpu_custom_call" | custom-call | tf_op jit(solution)/shard_map/pallas_call | solution.py:129
  114.0 1.2 fusion.67
  116.0 1.5 collective-permute-start.1
  118.7 15.2 %collective-permute-done.6 = f32[64,384]{1,0:T(8,128)S(1)} collective-permute-done((f32[64,384]{1,0:T(8,128)S(1)}, f32[64,384]{1,0:T(8,128)S(1)}, u32[]{:S(2)}, u32[]{:S(2)}) %collective-permute-start.6) | collective-permute-done | bytes 98336 | tf_op jit(solution)/shard_map/ppermute | solution.py:25
  134.7 4.9 %shard_map.63 = f32[128,128]{1,0:T(8,128)} custom-call(f32[128,128]{1,0:T(8,128)} %slice_add_fusion.1.a_ref), custom_call_target="tpu_custom_call" | custom-call | tf_op jit(solution)/shard_map/pallas_call | solution.py:129
  139.5 1.1 fusion.69
  140.6 1.1 fusion.145
  142.2 3.1 %collective-permute-start.2 = (f32[256,256]{1,0:T(8,128)S(1)}, f32[256,256]{1,0:T(8,128)S(1)}, u32[]{:S(2)}, u32[]{:S(2)}) collective-permute-start(f32[256,256]{1,0:T(8,128)S(1)} %slice_subtract_fusion.1), channel_id=1, source_target_pairs={{0,16},{4,20},{8,24},{12,28},{16,0},{20,4},{24,8},{28,12},{32,48},... | collective-permute-start | bytes 786440 | tf_op jit(solution)/shard_map/ppermute | solution.py:25
  146.1 6.9 %collective-permute-done.7 = f32[64,256]{1,0:T(8,128)S(1)} collective-permute-done((f32[64,256]{1,0:T(8,128)S(1)}, f32[64,256]{1,0:T(8,128)S(1)}, u32[]{:S(2)}, u32[]{:S(2)}) %collective-permute-start.7) | collective-permute-done | bytes 65568 | tf_op jit(solution)/shard_map/ppermute | solution.py:25
  153.8 4.9 %shard_map.64 = f32[128,128]{1,0:T(8,128)} custom-call(f32[128,128]{1,0:T(8,128)} %slice_add_fusion.a_ref), custom_call_target="tpu_custom_call" | custom-call | tf_op jit(solution)/shard_map/pallas_call | solution.py:129
  158.7 1.1 fusion.132
  160.1 1.6 collective-permute-start.3
  162.8 1.6 collective-permute-done.3
  164.4 3.2 %collective-permute-start.4 = (f32[128,128]{1,0:T(8,128)S(1)}, f32[128,128]{1,0:T(8,128)S(1)}, u32[]{:S(2)}, u32[]{:S(2)}) collective-permute-start(f32[128,128]{1,0:T(8,128)S(1)} %add.78), channel_id=1, source_target_pairs={{0,64},{4,68},{8,72},{12,76},{16,80},{20,84},{24,88},{28,92},{32,9... | collective-permute-start | bytes 196616 | tf_op jit(solution)/shard_map/ppermute | solution.py:25
  167.9 1.4 collective-permute-start.8
  169.2 2.7 %collective-permute-done.8 = f32[64,128]{1,0:T(8,128)S(1)} collective-permute-done((f32[64,128]{1,0:T(8,128)S(1)}, f32[64,128]{1,0:T(8,128)S(1)}, u32[]{:S(2)}, u32[]{:S(2)}) %collective-permute-start.8) | collective-permute-done | bytes 32800 | tf_op jit(solution)/shard_map/ppermute | solution.py:25
  173.5 4.8 %shard_map.65 = f32[128,128]{1,0:T(8,128)} custom-call(f32[128,128]{1,0:T(8,128)} %select_add_fusion.a_ref), custom_call_target="tpu_custom_call" | custom-call | tf_op jit(solution)/shard_map/pallas_call | solution.py:129
  179.4 1.1 fusion.158
  184.8 7.0 %shard_map.66 = f32[64,8192]{1,0:T(8,128)} custom-call(s32[64,128]{1,0:T(8,128)} %bitcast.206, f32[5,8192]{1,0:T(8,128)} %amp_ref.3, bf16[320,512]{1,0:T(8,128)(2,1)} %copy-done.5), custom_call_target="tpu_custom_call" | custom-call | tf_op jit(solution)/shard_map/pallas_call | solution.py:197
  (115 shorter events, 31.3 us)
Async XLA Ops:
  6.5 98.0 %all-reduce.2.cloned.1.call-start = ((), (), s32[]{:S(2)}) async-start(), calls=%async_computation | async-start | bytes 327680 | tf_op jit(solution)/shard_map/psum | solution.py:166
  7.7 25.3 %copy-start = (bf16[5,512,128]{2,1,0:T(8,128)(2,1)S(1)}, bf16[5,512,128]{2,1,0:T(8,128)(2,1)}, u32[]{:S(2)}) copy-start(bf16[5,512,128]{2,1,0:T(8,128)(2,1)} %table_ref.1) | copy-start | bytes 1966084
  37.1 4.9 %copy-start.17 = (f32[5,128]{1,0:T(8,128)S(1)}, f32[5,128]{1,0:T(8,128)}, u32[]{:S(2)}) copy-start(f32[5,128]{1,0:T(8,128)} %param.21) | copy-start | bytes 7684
  56.6 3.6 %copy-start.8 = (f32[128,128]{0,1:T(8,128)S(1)}, f32[128,128]{0,1:T(8,128)}, u32[]{:S(2)}) copy-start(f32[128,128]{0,1:T(8,128)} %copy.6) | copy-start | bytes 196612
  56.6 3.6 %copy-start.9 = (f32[128,128]{0,1:T(8,128)S(1)}, f32[128,128]{0,1:T(8,128)}, u32[]{:S(2)}) copy-start(f32[128,128]{0,1:T(8,128)} %copy.7) | copy-start | bytes 196612
  56.6 3.7 %copy-start.10 = (f32[128,128]{0,1:T(8,128)S(1)}, f32[128,128]{0,1:T(8,128)}, u32[]{:S(2)}) copy-start(f32[128,128]{0,1:T(8,128)} %copy.8) | copy-start | bytes 196612
  56.6 3.7 %copy-start.7 = (f32[128,128]{0,1:T(8,128)S(1)}, f32[128,128]{0,1:T(8,128)}, u32[]{:S(2)}) copy-start(f32[128,128]{0,1:T(8,128)} %copy.9) | copy-start | bytes 196612
  56.6 4.2 %copy-start.6 = (f32[128,128]{0,1:T(8,128)S(1)}, f32[128,128]{0,1:T(8,128)}, u32[]{:S(2)}) copy-start(f32[128,128]{0,1:T(8,128)} %copy.18) | copy-start | bytes 196612
  56.6 4.2 %copy-start.11 = (f32[128,128]{0,1:T(8,128)S(1)}, f32[128,128]{0,1:T(8,128)}, u32[]{:S(2)}) copy-start(f32[128,128]{0,1:T(8,128)} %copy.13) | copy-start | bytes 196612
  56.7 4.2 %copy-start.12 = (f32[128,128]{0,1:T(8,128)S(1)}, f32[128,128]{0,1:T(8,128)}, u32[]{:S(2)}) copy-start(f32[128,128]{0,1:T(8,128)} %copy.16) | copy-start | bytes 196612
  60.9 43.6 %copy-start.1 = (f32[128,128]{1,0:T(8,128)S(1)}, f32[128,128]{1,0:T(8,128)}, u32[]{:S(2)}) copy-start(f32[128,128]{1,0:T(8,128)} %shard_map.61) | copy-start | bytes 196612
  62.0 45.1 %collective-permute-start = (f32[512,512]{1,0:T(8,128)S(1)}, f32[512,512]{1,0:T(8,128)}, u32[]{:S(2)}, u32[]{:S(2)}) collective-permute-start(f32[512,512]{1,0:T(8,128)S(1)} %convolution_subtract_fusion), channel_id=1, source_target_pairs={{0,4},{4,0},{8,12},{12,8},{16,20},{20,16},{24,28},{28,24},{32,36},... | collective-permute-start | bytes 3145736 | tf_op jit(solution)/shard_map/ppermute | solution.py:25
  106.7 1.7 copy-start.16
  106.7 10.8 %collective-permute-start.5 = (f32[64,512]{1,0:T(8,128)S(1)}, f32[64,512]{1,0:T(8,128)S(1)}, u32[]{:S(2)}, u32[]{:S(2)}) collective-permute-start(f32[64,512]{1,0:T(8,128)S(1)} %convolution_subtract_fusion.1), channel_id=1, source_target_pairs={{0,4},{4,0},{8,12},{12,8},{16,20},{20,16},{24,28},{28,24},{32,36},... | collective-permute-start | bytes 393224 | tf_op jit(solution)/shard_map/ppermute | solution.py:25
  114.0 3.5 %copy-start.2 = (f32[128,128]{1,0:T(8,128)S(1)}, f32[128,128]{1,0:T(8,128)}, u32[]{:S(2)}) copy-start(f32[128,128]{1,0:T(8,128)} %shard_map.62) | copy-start | bytes 196612
  116.0 17.9 %collective-permute-start.1 = (f32[384,384]{1,0:T(8,128)S(1)}, f32[384,384]{1,0:T(8,128)S(1)}, u32[]{:S(2)}, u32[]{:S(2)}) collective-permute-start(f32[384,384]{1,0:T(8,128)S(1)} %slice_subtract_fusion), channel_id=1, source_target_pairs={{0,8},{4,12},{8,0},{12,4},{16,24},{20,28},{24,16},{28,20},{32,40},... | collective-permute-start | bytes 1769480 | tf_op jit(solution)/shard_map/ppermute | solution.py:25
  117.5 16.4 %copy-start.15 = (f32[128]{0:T(128)S(1)}, f32[128]{0:T(128)}, u32[]{:S(2)}) copy-start(f32[128]{0:T(128)} %get-tuple-element.93) | copy-start | bytes 1540
  118.1 15.8 %collective-permute-start.6 = (f32[64,384]{1,0:T(8,128)S(1)}, f32[64,384]{1,0:T(8,128)S(1)}, u32[]{:S(2)}, u32[]{:S(2)}) collective-permute-start(f32[64,384]{1,0:T(8,128)S(1)} %slice_subtract_fusion.2), channel_id=1, source_target_pairs={{0,8},{4,12},{8,0},{12,4},{16,24},{20,28},{24,16},{28,20},{32,40},... | collective-permute-start | bytes 294920 | tf_op jit(solution)/shard_map/ppermute | solution.py:25
  134.7 18.4 %copy-start.14 = (f32[128]{0:T(128)S(1)}, f32[128]{0:T(128)}, u32[]{:S(2)}) copy-start(f32[128]{0:T(128)} %get-tuple-element.96) | copy-start | bytes 1540
  142.2 30.7 %copy-start.13 = (f32[128]{0:T(128)S(1)}, f32[128]{0:T(128)}, u32[]{:S(2)}) copy-start(f32[128]{0:T(128)} %get-tuple-element.92) | copy-start | bytes 1540
  142.2 10.8 %collective-permute-start.2 = (f32[256,256]{1,0:T(8,128)S(1)}, f32[256,256]{1,0:T(8,128)S(1)}, u32[]{:S(2)}, u32[]{:S(2)}) collective-permute-start(f32[256,256]{1,0:T(8,128)S(1)} %slice_subtract_fusion.1), channel_id=1, source_target_pairs={{0,16},{4,20},{8,24},{12,28},{16,0},{20,4},{24,8},{28,12},{32,48},... | collective-permute-start | bytes 786440 | tf_op jit(solution)/shard_map/ppermute | solution.py:25
  145.4 7.6 %collective-permute-start.7 = (f32[64,256]{1,0:T(8,128)S(1)}, f32[64,256]{1,0:T(8,128)S(1)}, u32[]{:S(2)}, u32[]{:S(2)}) collective-permute-start(f32[64,256]{1,0:T(8,128)S(1)} %slice_subtract_fusion.3), channel_id=1, source_target_pairs={{0,16},{4,20},{8,24},{12,28},{16,0},{20,4},{24,8},{28,12},{32,48},... | collective-permute-start | bytes 196616 | tf_op jit(solution)/shard_map/ppermute | solution.py:25
  153.8 27.8 %copy-start.3 = (f32[128,128]{1,0:T(8,128)S(1)}, f32[128,128]{1,0:T(8,128)}, u32[]{:S(2)}) copy-start(f32[128,128]{1,0:T(8,128)} %shard_map.63) | copy-start | bytes 196612
  158.7 22.4 %copy-start.4 = (f32[128,128]{1,0:T(8,128)S(1)}, f32[128,128]{1,0:T(8,128)}, u32[]{:S(2)}) copy-start(f32[128,128]{1,0:T(8,128)} %shard_map.64) | copy-start | bytes 196612
  160.1 4.3 %collective-permute-start.3 = (f32[128,128]{1,0:T(8,128)S(1)}, f32[128,128]{1,0:T(8,128)S(1)}, u32[]{:S(2)}, u32[]{:S(2)}) collective-permute-start(f32[128,128]{1,0:T(8,128)S(1)} %slice_subtract_fusion.4), channel_id=1, source_target_pairs={{0,32},{4,36},{8,40},{12,44},{16,48},{20,52},{24,56},{28,60},{32,0... | collective-permute-start | bytes 196616 | tf_op jit(solution)/shard_map/ppermute | solution.py:25
  164.4 8.4 %collective-permute-start.4 = (f32[128,128]{1,0:T(8,128)S(1)}, f32[128,128]{1,0:T(8,128)S(1)}, u32[]{:S(2)}, u32[]{:S(2)}) collective-permute-start(f32[128,128]{1,0:T(8,128)S(1)} %add.78), channel_id=1, source_target_pairs={{0,64},{4,68},{8,72},{12,76},{16,80},{20,84},{24,88},{28,92},{32,9... | collective-permute-start | bytes 196616 | tf_op jit(solution)/shard_map/ppermute | solution.py:25
  167.9 4.0 %collective-permute-start.8 = (f32[64,128]{1,0:T(8,128)S(1)}, f32[64,128]{1,0:T(8,128)S(1)}, u32[]{:S(2)}, u32[]{:S(2)}) collective-permute-start(f32[64,128]{1,0:T(8,128)S(1)} %slice_subtract_fusion.5), channel_id=1, source_target_pairs={{0,32},{4,36},{8,40},{12,44},{16,48},{20,52},{24,56},{28,60},{32,0... | collective-permute-start | bytes 98312 | tf_op jit(solution)/shard_map/ppermute | solution.py:25
  171.9 6.5 %collective-permute-start.9 = (f32[64,128]{1,0:T(8,128)S(1)}, f32[64,128]{1,0:T(8,128)S(1)}, u32[]{:S(2)}, u32[]{:S(2)}) collective-permute-start(f32[64,128]{1,0:T(8,128)S(1)} %add.84), channel_id=1, source_target_pairs={{0,64},{4,68},{8,72},{12,76},{16,80},{20,84},{24,88},{28,92},{32,9... | collective-permute-start | bytes 98312 | tf_op jit(solution)/shard_map/ppermute | solution.py:25
  184.1 0.7 copy-start.5
Sparse Core Ops, SparseCore 0:
  62.2 42.2 all-reduce.1
where the time goes:
time: 200 us; the launch traced here: 199 us
  waiting for transfers between devices  68.9 us (34%)
  Pallas kernels  38.5 us (19%)
  matrix products  27.4 us (14%)
  blocking collectives  18 us (9%)
  between operations  14 us (7%)
  starting transfers between devices  13.4 us (7%)
  local copies, waits for them, and re-layouts  12.9 us (6%)
  other arithmetic  5.62 us (3%)
    psum x1, waiting for transfers between devices, shards(): w, rhs_rows = lax.psum((w, c), 'obs')  42.5 us
    ppermute x10, waiting for transfers between devices, swapped(): return lax.ppermute(value, axis, pairs)  26.4 us
    pallas_call x5, Pallas kernels, inverse_factor(): pl.pallas_call(inverse_factor_kernel, out_shape=jax.ShapeDtypeStruct((n,...  24.3 us
    psum x1, blocking collectives, shards(): w, rhs_rows = lax.psum((w, c), 'obs')  18 us
    dot_general x31, matrix products, dot(): return jnp.dot(a, b, precision=highest)  17.9 us
    ppermute x10, starting transfers between devices, swapped(): return lax.ppermute(value, axis, pairs)  13.4 us
    dot_general x15, matrix products, shards(): jnp.einsum('pk,pl->kl', table[t] * w[PAIR_ROW[s, t]][:, None], table[s],...  9.55 us
    dot_general x10, local copies, waits for them, and re-layouts, shards(): jnp.einsum('pk,pl->kl', table[t] * w[PAIR_ROW[s, t]][:, None], table[s],...  8.87 us
  transfers between devices with their start and end apart: 11, of which 5 were waited for; matrix products, arithmetic and copies ran while one was open for 4% of the time, Pallas kernels for 5%

commit v1 on v0

--- a/solution.py
+++ b/solution.py
@@ -17,12 +17,6 @@
 
 def iota(shape, axis):
     return lax.broadcasted_iota(jnp.int32, shape, axis)
-
-
-def swapped(value, axis, stride):
-    mask = 2**stride
-    pairs = [(source, source ^ mask) for source in range(lax.axis_size(axis))]
-    return lax.ppermute(value, axis, pairs)
 
 
 def amplitude_products(amp):
@@ -73,7 +67,7 @@
         hi = v.astype(bf16)
         lo = (v - hi.astype(f32)).astype(bf16)
         both = jnp.dot(jnp.concatenate([hi, lo], axis=0), table_ref[t], preferred_element_type=f32)
-        c_ref[:, t * knots:(t + 1) * knots] = both[:nf] + both[nf:]
+        c_ref[t] = both[:nf] + both[nf:]
 
 
 def fit_kernel(pattern_ref, amp_ref, f_ref, out_ref):
@@ -87,10 +81,10 @@
     out_ref[...] = total
 
 
-def inverse_factor_kernel(a_ref, o_ref, m_ref, q_ref):
-    n = a_ref.shape[0]
+def inverse_factor(a, o_ref, m_ref, q_ref):
+    n = a.shape[0]
     sub, lane, lane2 = iota((PANEL, n), 0), iota((PANEL, n), 1), iota((n, n), 1)
-    m_ref[...] = a_ref[...]
+    m_ref[...] = a
     q_ref[...] = jnp.zeros((n, n), f32)
 
     def body(b, carry):
@@ -124,75 +118,223 @@
     lax.fori_loop(0, n // PANEL, body, 0)
 
 
-def inverse_factor(a):
-    n = a.shape[0]
-    return pl.pallas_call(
-        inverse_factor_kernel,
-        out_shape=jax.ShapeDtypeStruct((n, n), f32),
-        scratch_shapes=[pltpu.VMEM((n, n), f32)] * 2,
-    )(a)
-
-
-def add_prior(matrix, prior_precision, tier_index):
-    offset = tier_index * prior_precision.shape[1]
-    return matrix.at[offset:, offset:].add(jnp.diag(prior_precision[tier_index]))
-
-
 def dot(a, b):
-    return jnp.dot(a, b, precision=highest)
-
-
-def eliminate(matrix, rhs_rows, tier_index, knot_count):
-    offset = tier_index * knot_count
-    factor = inverse_factor(matrix[offset:, offset:])
-    whiten = dot(factor, rhs_rows[:, offset:].T)
-    coupling = dot(factor, matrix[offset:, :offset])
-    schur_part = matrix[:offset, :offset] - dot(coupling.T, coupling)
-    reduced = rhs_rows[:, :offset] - dot(whiten.T, coupling)
-    return (factor, coupling, whiten, schur_part, reduced)
+    return jnp.dot(a, b, precision=highest, preferred_element_type=f32)
+
+
+def dot_nt(a, b):
+    return lax.dot_general(a, b, (((1,), (1,)), ((), ())), precision=highest, preferred_element_type=f32)
+
+
+def split2(v):
+    hi = v.astype(bf16)
+    return jnp.concatenate([hi, (v - hi.astype(f32)).astype(bf16)], axis=0)
+
+
+def tri(t, s):
+    return t * (t + 1) // 2 + s
+
+
+def tree_kernel(wpart_ref, cpart_ref, table_ref, prior_ref, out_ref,
+                bt_ref, wall_ref, cpiece_ref, csum_ref, g_ref, linv_ref, x_ref, z_ref, wt_ref, m_ref, q_ref,
+                s4, s4r, c4, c4r, s3, s3r, c3, c3r, s2, s2r, c2, c2r, s1, s1r, c1, c1r, send_sem, recv_sem):
+    tiers, patterns, knots = table_ref.shape
+    nf = cpart_ref.shape[1]
+    top = tiers - 1
+    region, obs = lax.axis_index("region"), lax.axis_index("obs")
+    n_obs = 4
+    quarter = nf // n_obs
+    own = {4: s4, 3: s3, 2: s2, 1: s1}
+    got = {4: s4r, 3: s3r, 2: s2r, 1: s1r}
+    cown = {4: c4, 3: c3, 2: c2, 1: c1}
+    cgot = {4: c4r, 3: c3r, 2: c2r, 1: c1r}
+    y_peers = [(region, lax.rem(obs + d, n_obs)) for d in range(1, n_obs)]
+
+    def flip(*bits):
+        other = region
+        for bit in bits:
+            other = other + bit - 2 * bit * lax.rem(lax.div(region, bit), 2)
+        return other, obs
+
+    tree_peer = {4: flip(1), 3: flip(2), 2: flip(2, 4)}
+    z_peers = [flip(8), flip(8, 16), flip(16)]
+    started = []
+
+    def send(src, dst, k, dev):
+        copy = pltpu.make_async_remote_copy(
+            src_ref=src, dst_ref=dst, send_sem=send_sem.at[k], recv_sem=recv_sem.at[k],
+            device_id=dev, device_id_type=pl.DeviceIdType.MESH)
+        copy.start()
+        started.append(copy)
+        return copy
+
+    barrier = pltpu.get_barrier_semaphore()
+    peers = y_peers + list(tree_peer.values()) + z_peers
+    for dev in peers:
+        pl.semaphore_signal(barrier, inc=1, device_id=dev, device_id_type=pl.DeviceIdType.MESH)
+    wall_ref[obs] = wpart_ref[...]
+    pl.semaphore_wait(barrier, len(peers))
+
+    w_copies = [send(wall_ref.at[obs], wall_ref.at[obs], k, dev) for k, dev in enumerate(y_peers)]
+    rs_copies = [
+        send(cpart_ref.at[:, pl.ds(pl.multiple_of(dev[1] * quarter, quarter), quarter), :], cpiece_ref.at[k], 3 + k, dev)
+        for k, dev in enumerate(y_peers)
+    ]
+    for t in range(tiers):
+        bt_ref[t] = table_ref[t].astype(f32).T.astype(bf16)
+    for copy in w_copies:
+        copy.wait_recv()
+    w = (wall_ref[0] + wall_ref[1]) + (wall_ref[2] + wall_ref[3])
+    for t in range(top, -1, -1):
+        for s in range(t, -1, -1):
+            row = PAIR_ROW[(s, t)]
+            scaled = bt_ref[t].astype(f32) * w[row:row + 1, :]
+            both = lax.dot_general(split2(scaled), bt_ref[s], (((1,), (1,)), ((), ())), preferred_element_type=f32)
+            g_ref[tri(t, s)] = both[:knots] + both[knots:]
+    for copy in rs_copies:
+        copy.wait_recv()
+    mine = pl.ds(pl.multiple_of(obs * quarter, quarter), quarter)
+    csum_ref[:, mine, :] = cpart_ref[:, mine, :] + cpiece_ref[0] + cpiece_ref[1] + cpiece_ref[2]
+    ag_copies = [
+        send(csum_ref.at[:, mine, :], csum_ref.at[:, mine, :], 6 + k, dev) for k, dev in enumerate(y_peers)
+    ]
+
+    eye = iota((knots, knots), 0) == iota((knots, knots), 1)
+
+    def factor(t, block):
+        inverse_factor(block + jnp.where(eye, prior_ref[t:t + 1, :], 0.0), linv_ref.at[t], m_ref, q_ref)
+
+    def eliminate(t, g, c, sem, before_rest, before_c):
+        factor(t, g(t, t))
+        linv = linv_ref[t]
+        last = t - 1
+        before_rest()
+        xl = dot(linv, g(t, last))
+        x_ref[tri(t - 1, last)] = xl
+        own[t][tri(last, last)] = g(last, last) - dot(xl.T, xl)
+        copies = []
+        n_tri = tri(last, last)
+        devs = z_peers if t == 1 else [tree_peer[t]]
+        for k, dev in enumerate(devs):
+            dst = got[t].at[k] if t == 1 else got[t].at[n_tri]
+            copies.append(send(own[t].at[n_tri], dst, sem + k, dev))
+        xs = [xl]
+        if last:
+            rest = dot(linv, jnp.concatenate([g(t, s) for s in range(last)], axis=1))
+            xs = [rest[:, s * knots:(s + 1) * knots] for s in range(last)] + [xl]
+            for s in range(last):
+                x_ref[tri(t - 1, s)] = xs[s]
+            for u in range(last, -1, -1):
+                width = min(u + 1, last)
+                prod = dot(xs[u].T, rest[:, :width * knots])
+                for s in range(width):
+                    own[t][tri(u, s)] = g(u, s) - prod[:, s * knots:(s + 1) * knots]
+            for src, dst, k, dev in rest_parts(t, n_tri, sem):
+                copies.append(send(src, dst, k, dev))
+        before_c()
+        z = dot_nt(c(t), linv)
+        z_ref[t] = z
+        red = dot(z, jnp.concatenate(xs, axis=1))
+        for s in range(t):
+            cown[t][s] = c(s) - red[:, s * knots:(s + 1) * knots]
+        if t == 1:
+            for k, dev in enumerate(devs):
+                copies.append(send(cown[t].at[0], cgot[t].at[k], sem + 3 + k, dev))
+        elif t == 3:
+            part = pl.ds(pl.multiple_of(core * (nf // 2), nf // 2), nf // 2)
+            copies.append(send(cown[t].at[:, part, :], cgot[t].at[:, part, :], sem + 2, devs[0]))
+        else:
+            copies.append(send(cown[t], cgot[t], sem + 2, devs[0]))
+        return copies
+
+    core = lax.rem(region, 2)
+    half = pl.ds(pl.multiple_of(core * (knots // 2), knots // 2), knots // 2)
+
+    def rest_parts(t, n_tri, sem):
+        if t == 3:
+            return [(own[t].at[pl.ds(0, n_tri), half, :], got[t].at[pl.ds(0, n_tri), half, :], sem + 1, tree_peer[t])]
+        return [(own[t].at[pl.ds(0, n_tri)], got[t].at[pl.ds(0, n_tri)], sem + 1, tree_peer[t])]
+
+    nothing = lambda: None
+
+    def wait_ag():
+        for copy in ag_copies:
+            copy.wait_recv()
+
+    e4 = eliminate(4, lambda t, s: g_ref[tri(t, s)], lambda s: csum_ref[s], 9, nothing, wait_ag)
+
+    def summed(t):
+        return lambda u, s: own[t][tri(u, s)] + got[t][tri(u, s)]
+
+    def csummed(t):
+        return lambda s: cown[t][s] + cgot[t][s]
+
+    e4[0].wait_recv()
+    e3 = eliminate(3, summed(4), csummed(4), 12, e4[1].wait_recv, e4[2].wait_recv)
+    e3[0].wait_recv()
+    relays = []
+
+    def relay_rest():
+        e3[1].wait_recv()
+        part = got[3].at[pl.ds(0, 5), half, :]
+        relays.append(send(part, part, 15, tree_peer[4]))
+        e3[2].wait_recv()
+        fields = pl.ds(pl.multiple_of(core * (nf // 2), nf // 2), nf // 2)
+        part = cgot[3].at[:, fields, :]
+        relays.append(send(part, part, 16, tree_peer[4]))
+        relays[0].wait_recv()
+
+    e2 = eliminate(2, summed(3), csummed(3), 17, relay_rest, lambda: relays[1].wait_recv())
+    e2[0].wait_recv()
+    e1 = eliminate(1, summed(2), csummed(2), 20, e2[1].wait_recv, e2[2].wait_recv)
+    for copy in e1[:3]:
+        copy.wait_recv()
+    factor(0, (own[1][0] + got[1][0]) + (got[1][1] + got[1][2]))
+    linv = linv_ref[0]
+    for copy in e1[3:]:
+        copy.wait_recv()
+    c0 = (cown[1][0] + cgot[1][0]) + (cgot[1][1] + cgot[1][2])
+    wts = [dot(dot_nt(c0, linv), linv)]
+    for t in range(1, tiers):
+        x = jnp.concatenate([x_ref[tri(t - 1, s)] for s in range(t)], axis=1)
+        target = z_ref[t] - dot_nt(jnp.concatenate(wts, axis=1), x)
+        wts.append(dot(target, linv_ref[t]))
+    for t in range(tiers):
+        both = jnp.dot(split2(wts[t]), bt_ref[t], preferred_element_type=f32)
+        out_ref[t * nf:(t + 1) * nf, :] = (both[:nf] + both[nf:]).astype(bf16)
+    for copy in started:
+        copy.wait_send()
 
 
 def shards(pattern, amplitude, basis_table, fields, prior_precision):
     tiers, patterns, knots = basis_table.shape
-    ancestors = tiers - 1
     obs = pattern.shape[0]
     nf = fields.shape[0]
     pattern2 = pattern.reshape(obs // 128, 128)
     w, c = pl.pallas_call(
         functools.partial(stats_kernel, chunk=1024),
-        out_shape=(jax.ShapeDtypeStruct((16, patterns), f32), jax.ShapeDtypeStruct((nf, tiers * knots), f32)),
+        out_shape=(jax.ShapeDtypeStruct((16, patterns), f32), jax.ShapeDtypeStruct((tiers, nf, knots), f32)),
         scratch_shapes=[pltpu.VMEM((tiers * nf + 32, patterns), f32)],
     )(pattern2, amplitude, basis_table, fields)
-    w, rhs_rows = lax.psum((w, c), "obs")
-    table = basis_table.astype(f32)
-    blocks = [[None] * tiers for _ in range(tiers)]
-    for s in range(tiers):
-        for t in range(s, tiers):
-            blk = jnp.einsum("pk,pl->kl", table[t] * w[PAIR_ROW[(s, t)]][:, None], table[s], precision=highest)
-            blocks[t][s] = blk
-            blocks[s][t] = blk.T if t > s else blk
-    matrix = jnp.concatenate([jnp.concatenate(row, axis=1) for row in blocks], axis=0)
-    matrix = add_prior(matrix, prior_precision, ancestors)
-    region_bits = lax.axis_size("region").bit_length() - 1
-    stored = {}
-    for tier_index in range(ancestors, 0, -1):
-        factor, coupling, whiten, schur_part, reduced = eliminate(matrix, rhs_rows, tier_index, knots)
-        stored[tier_index] = (factor, coupling, whiten)
-        bits = [ancestors - tier_index] if tier_index > 1 else range(ancestors - 1, region_bits)
-        for bit in bits:
-            other_mat, other_rhs = swapped((schur_part, reduced), "region", bit)
-            schur_part = schur_part + other_mat
-            reduced = reduced + other_rhs
-        matrix = add_prior(schur_part, prior_precision, tier_index - 1)
-        rhs_rows = reduced
-    root = inverse_factor(matrix)
-    path = dot(root.T, dot(root, rhs_rows.T))
-    for tier_index in range(1, tiers):
-        factor, coupling, whiten = stored[tier_index]
-        path = jnp.concatenate([path, dot(factor.T, whiten - dot(coupling, path))], axis=0)
-    per_pattern = jnp.concatenate(
-        [dot(path[t * knots:(t + 1) * knots].T, table[t].T) for t in range(tiers)], axis=0
-    ).astype(bf16)
+    block = lambda n: pltpu.VMEM((n, knots, knots), f32)
+    rhs = lambda n: pltpu.VMEM((n, nf, knots), f32)
+    per_pattern = pl.pallas_call(
+        tree_kernel,
+        out_shape=jax.ShapeDtypeStruct((tiers * nf, patterns), bf16),
+        scratch_shapes=[
+            pltpu.VMEM((tiers, knots, patterns), bf16),
+            pltpu.VMEM((4, 16, patterns), f32),
+            pltpu.VMEM((3, tiers, nf // 4, knots), f32),
+            rhs(tiers), block(15), block(5), block(10), rhs(5), rhs(5),
+            pltpu.VMEM((knots, knots), f32), pltpu.VMEM((knots, knots), f32),
+            block(10), block(10), rhs(4), rhs(4),
+            block(6), block(6), rhs(3), rhs(3),
+            block(3), block(3), rhs(2), rhs(2),
+            block(1), block(3), rhs(1), rhs(3),
+            pltpu.SemaphoreType.DMA((26,)), pltpu.SemaphoreType.DMA((26,)),
+        ],
+        compiler_params=pltpu.CompilerParams(collective_id=0, has_side_effects=True),
+    )(w, c, basis_table, prior_precision)
     chunk = min(1024, obs)
     return pl.pallas_call(
         fit_kernel,

time: 200 us -> 69.4 us (0.35)
  the two profiles are of different devices: /device:TPU:0 before, /device:TPU:1 now
where the time goes in v1:
time: 69.4 us; the launch traced here: 68.7 us
  Pallas kernels  68.7 us (99%)
    pallas_call x1, Pallas kernels, shards(): pl.pallas_call(tree_kernel, out_shape=jax.ShapeDtypeStruct((tiers * nf, p...  54.5 us
    pallas_call x1, Pallas kernels, shards(): pl.pallas_call(functools.partial(stats_kernel, chunk=1024), out_shape=(ja...  7.18 us
    pallas_call x1, Pallas kernels, shards(): pl.pallas_call(fit_kernel, grid=(obs // chunk,), in_specs=[pl.BlockSpec((...  7.04 us

profile of v1, /device:TPU:1, one launch (start us, length us, event | category | flops | bytes accessed | tf_op | source)
XLA Modules:
  0.0 68.7 jit_solution(7143332719110765977)
XLA Ops:
  0.0 7.2 %shard_map.55 = (f32[16,512]{1,0:T(8,128)}, f32[5,64,128]{2,1,0:T(8,128)}) custom-call(s32[64,128]{1,0:T(8,128)} %bitcast.1, f32[5,8192]{1,0:T(8,128)} %amp_ref.3, bf16[5,512,128]{2,1,0:T(8,128)(2,1)} %table_ref.3, bf16[64,8192]{1,0:T(8,128)(2,1)} %fields_ref.1), custom_call_target="tpu_custom_call" | custom-call | tf_op jit(solution)/shard_map/pallas_call | solution.py:314
  7.2 54.5 %shard_map.56.f_ref = bf16[320,512]{1,0:T(8,128)(2,1)} custom-call(f32[16,512]{1,0:T(8,128)} %get-tuple-element.7.wpart_ref, f32[5,64,128]{2,1,0:T(8,128)} %get-tuple-element.8.cpart_ref, bf16[5,512,128]{2,1,0:T(8,128)(2,1)} %table_ref.3, f32[5,128]{1,0:T(8,128)} %prior_ref.1), custom_call_target="tpu_custom_call" | custom-call | tf_op jit(solution)/shard_map/pallas_call | solution.py:321
  61.7 7.0 %shard_map.57 = f32[64,8192]{1,0:T(8,128)} custom-call(s32[64,128]{1,0:T(8,128)} %bitcast.2, f32[5,8192]{1,0:T(8,128)} %amp_ref.3, bf16[320,512]{1,0:T(8,128)(2,1)} %shard_map.56.f_ref), custom_call_target="tpu_custom_call" | custom-call | tf_op jit(solution)/shard_map/pallas_call | solution.py:339

commit v2 on v1

--- a/solution.py
+++ b/solution.py
@@ -40,10 +40,9 @@
     return jnp.concatenate(parts, axis=1)
 
 
-def stats_kernel(pattern_ref, amp_ref, table_ref, fields_ref, w_ref, c_ref, acc_ref, *, chunk):
-    tiers, patterns, knots = table_ref.shape
-    obs = amp_ref.shape[1]
-    nf = fields_ref.shape[0]
+def accumulate(pattern_ref, amp_ref, fields_ref, acc_ref, chunk):
+    tiers, obs = amp_ref.shape
+    patterns = acc_ref.shape[1]
     acc_ref[...] = jnp.zeros_like(acc_ref)
 
     def step(i, carry):
@@ -60,14 +59,6 @@
         return carry
 
     lax.fori_loop(0, obs // chunk, step, 0)
-    base = tiers * nf
-    w_ref[...] = acc_ref[base:base + 16, :] + acc_ref[base + 16:base + 32, :]
-    for t in range(tiers):
-        v = acc_ref[t * nf:(t + 1) * nf, :]
-        hi = v.astype(bf16)
-        lo = (v - hi.astype(f32)).astype(bf16)
-        both = jnp.dot(jnp.concatenate([hi, lo], axis=0), table_ref[t], preferred_element_type=f32)
-        c_ref[t] = both[:nf] + both[nf:]
 
 
 def fit_kernel(pattern_ref, amp_ref, f_ref, out_ref):
@@ -81,41 +72,61 @@
     out_ref[...] = total
 
 
-def inverse_factor(a, o_ref, m_ref, q_ref):
+def split3(v):
+    hi = v.astype(bf16).astype(f32)
+    rest = v - hi
+    mid = rest.astype(bf16).astype(f32)
+    return hi, mid, rest - mid
+
+
+def inverse_factor(a, o_ref, m_ref, t_ref, tb_ref, q_ref):
     n = a.shape[0]
     sub, lane, lane2 = iota((PANEL, n), 0), iota((PANEL, n), 1), iota((n, n), 1)
+    zero = jnp.zeros((PANEL, n), f32)
     m_ref[...] = a
-    q_ref[...] = jnp.zeros((n, n), f32)
-
-    def body(b, carry):
+    tb_ref[...] = jnp.zeros((n, n), bf16)
+    q_ref[...] = jnp.zeros((n, n), bf16)
+
+    def body(b, rows):
         off = pl.multiple_of(b * PANEL, PANEL)
-        whole = m_ref[...]
-        rows = m_ref[pl.ds(off, PANEL), :]
+        prev = off - PANEL
         cols = [
             jnp.take_along_axis(rows, jnp.zeros((PANEL, n), jnp.int32) + (off + l), axis=1)
             for l in range(PANEL)
         ]
+        update = jnp.dot(tb_ref[...], q_ref[...], preferred_element_type=f32)
+        hi, mid, low = split3(rows)
+        turned = jnp.concatenate([rows, hi, hi, mid, hi, low, mid, zero], axis=0).T
+        t_ref[...] = turned
+        m_ref[...] = jnp.where((lane2 >= prev) & (lane2 < off), 0.0, m_ref[...]) - update
+        tb_ref[...] = turned.astype(bf16)
+        nxt = pl.multiple_of(jnp.minimum(off + PANEL, n - PANEL), PANEL)
+        after = m_ref[pl.ds(nxt, PANEL), :]
+        near = t_ref[pl.ds(nxt, PANEL), :]
+        coup = [jnp.broadcast_to(near[:, l:l + 1], (PANEL, n)) for l in range(PANEL)]
         inside = (lane >= off) & (lane < off + PANEL)
         x = jnp.where(lane - off == sub, 1.0, jnp.where(inside, 0.0, rows))
-        outs = x
+        outs = invs = x
         for j in range(PANEL):
             pick = lambda v: jnp.broadcast_to(v[j:j + 1, :], (PANEL, n))
-            pivot = pick(cols[j])
-            inv = 1.0 / pivot
+            inv = 1.0 / pick(cols[j])
             xj = pick(x)
-            outs = jnp.where(sub == j, xj * lax.rsqrt(pivot), outs)
-            mult = jnp.where(sub == j, inv, -cols[j] * inv)
+            invs = jnp.where(sub == j, inv, invs)
+            outs = jnp.where(sub == j, x, outs)
+            mult = jnp.where(sub == j, 0.0, cols[j] * inv)
             for l in range(j + 1, PANEL):
-                cols[l] = jnp.where(sub == j, 0.0, cols[l]) + mult * pick(cols[l])
-            x = jnp.where(sub == j, 0.0, x) + mult * xj
-        o_ref[pl.ds(off, PANEL), :] = jnp.where(lane - off <= sub, outs, 0.0)
-        q_ref[pl.ds(off, PANEL), :] = x
-        update = jnp.dot(whole, q_ref[...], precision=highest, preferred_element_type=f32)
-        q_ref[pl.ds(off, PANEL), :] = jnp.zeros((PANEL, n), f32)
-        m_ref[...] = jnp.where((lane2 >= off) & (lane2 < off + PANEL), 0.0, whole) - update
-        return carry
-
-    lax.fori_loop(0, n // PANEL, body, 0)
+                cols[l] = cols[l] - mult * pick(cols[l])
+            x = x - mult * xj
+        x = x * invs
+        o_ref[pl.ds(off, PANEL), :] = jnp.where(lane - off <= sub, outs * jnp.sqrt(invs), 0.0)
+        hi, mid, low = split3(x)
+        q_ref[...] = jnp.concatenate([zero, hi, mid, hi, low, hi, mid, zero], axis=0).astype(bf16)
+        terms = [coup[l] * jnp.broadcast_to(x[l:l + 1, :], (PANEL, n)) for l in range(PANEL)]
+        while len(terms) > 1:
+            terms = [terms[i] + terms[i + 1] for i in range(0, len(terms), 2)]
+        return jnp.where(inside, 0.0, after) - terms[0]
+
+    lax.fori_loop(0, n // PANEL, body, m_ref[0:PANEL, :])
 
 
 def dot(a, b):
@@ -135,11 +146,11 @@
     return t * (t + 1) // 2 + s
 
 
-def tree_kernel(wpart_ref, cpart_ref, table_ref, prior_ref, out_ref,
-                bt_ref, wall_ref, cpiece_ref, csum_ref, g_ref, linv_ref, x_ref, z_ref, wt_ref, m_ref, q_ref,
+def tree_kernel(pattern_ref, amp_ref, table_ref, fields_ref, prior_ref, out_ref,
+                acc_ref, cpart_ref, bt_ref, wall_ref, cpiece_ref, csum_ref, g_ref, linv_ref, x_ref, z_ref, m_ref, t_ref, tb_ref, q_ref,
                 s4, s4r, c4, c4r, s3, s3r, c3, c3r, s2, s2r, c2, c2r, s1, s1r, c1, c1r, send_sem, recv_sem):
     tiers, patterns, knots = table_ref.shape
-    nf = cpart_ref.shape[1]
+    nf = fields_ref.shape[0]
     top = tiers - 1
     region, obs = lax.axis_index("region"), lax.axis_index("obs")
     n_obs = 4
@@ -172,10 +183,16 @@
     peers = y_peers + list(tree_peer.values()) + z_peers
     for dev in peers:
         pl.semaphore_signal(barrier, inc=1, device_id=dev, device_id_type=pl.DeviceIdType.MESH)
-    wall_ref[obs] = wpart_ref[...]
+    accumulate(pattern_ref, amp_ref, fields_ref, acc_ref, 1024)
+    base = tiers * nf
+    wall_ref[obs] = acc_ref[base:base + 16, :] + acc_ref[base + 16:base + 32, :]
     pl.semaphore_wait(barrier, len(peers))
 
     w_copies = [send(wall_ref.at[obs], wall_ref.at[obs], k, dev) for k, dev in enumerate(y_peers)]
+    for t in range(tiers):
+        v = split2(acc_ref[t * nf:(t + 1) * nf, :])
+        both = jnp.dot(v, table_ref[t], preferred_element_type=f32)
+        cpart_ref[t] = both[:nf] + both[nf:]
     rs_copies = [
         send(cpart_ref.at[:, pl.ds(pl.multiple_of(dev[1] * quarter, quarter), quarter), :], cpiece_ref.at[k], 3 + k, dev)
         for k, dev in enumerate(y_peers)
@@ -202,7 +219,7 @@
     eye = iota((knots, knots), 0) == iota((knots, knots), 1)
 
     def factor(t, block):
-        inverse_factor(block + jnp.where(eye, prior_ref[t:t + 1, :], 0.0), linv_ref.at[t], m_ref, q_ref)
+        inverse_factor(block + jnp.where(eye, prior_ref[t:t + 1, :], 0.0), linv_ref.at[t], m_ref, t_ref, tb_ref, q_ref)
 
     def eliminate(t, g, c, sem, before_rest, before_c):
         factor(t, g(t, t))
@@ -311,22 +328,19 @@
     obs = pattern.shape[0]
     nf = fields.shape[0]
     pattern2 = pattern.reshape(obs // 128, 128)
-    w, c = pl.pallas_call(
-        functools.partial(stats_kernel, chunk=1024),
-        out_shape=(jax.ShapeDtypeStruct((16, patterns), f32), jax.ShapeDtypeStruct((tiers, nf, knots), f32)),
-        scratch_shapes=[pltpu.VMEM((tiers * nf + 32, patterns), f32)],
-    )(pattern2, amplitude, basis_table, fields)
     block = lambda n: pltpu.VMEM((n, knots, knots), f32)
     rhs = lambda n: pltpu.VMEM((n, nf, knots), f32)
     per_pattern = pl.pallas_call(
         tree_kernel,
         out_shape=jax.ShapeDtypeStruct((tiers * nf, patterns), bf16),
         scratch_shapes=[
+            pltpu.VMEM((tiers * nf + 32, patterns), f32), rhs(tiers),
             pltpu.VMEM((tiers, knots, patterns), bf16),
             pltpu.VMEM((4, 16, patterns), f32),
             pltpu.VMEM((3, tiers, nf // 4, knots), f32),
-            rhs(tiers), block(15), block(5), block(10), rhs(5), rhs(5),
+            rhs(tiers), block(15), block(5), block(10), rhs(5),
             pltpu.VMEM((knots, knots), f32), pltpu.VMEM((knots, knots), f32),
+            pltpu.VMEM((knots, knots), bf16), pltpu.VMEM((knots, knots), bf16),
             block(10), block(10), rhs(4), rhs(4),
             block(6), block(6), rhs(3), rhs(3),
             block(3), block(3), rhs(2), rhs(2),
@@ -334,7 +348,7 @@
             pltpu.SemaphoreType.DMA((26,)), pltpu.SemaphoreType.DMA((26,)),
         ],
         compiler_params=pltpu.CompilerParams(collective_id=0, has_side_effects=True),
-    )(w, c, basis_table, prior_precision)
+    )(pattern2, amplitude, basis_table, fields, prior_precision)
     chunk = min(1024, obs)
     return pl.pallas_call(
         fit_kernel,

time: 69.4 us -> 61.4 us (0.88)
  the two profiles are of different devices: /device:TPU:1 before, /device:TPU:0 now
where the time goes in v2:
time: 61.4 us; the launch traced here: 60.4 us
  Pallas kernels  60.4 us (98%)
    pallas_call x1, Pallas kernels, shards(): pl.pallas_call(tree_kernel, out_shape=jax.ShapeDtypeStruct((tiers * nf, p...  53.3 us
    pallas_call x1, Pallas kernels, shards(): pl.pallas_call(fit_kernel, grid=(obs // chunk,), in_specs=[pl.BlockSpec((...  7.04 us

profile of v2, /device:TPU:0, one launch (start us, length us, event | category | flops | bytes accessed | tf_op | source)
XLA Modules:
  0.0 60.4 jit_solution(14958774877449502000)
XLA Ops:
  0.0 53.3 %shard_map.55.f_ref = bf16[320,512]{1,0:T(8,128)(2,1)} custom-call(s32[64,128]{1,0:T(8,128)} %bitcast.1, f32[5,8192]{1,0:T(8,128)} %amp_ref.3, bf16[5,512,128]{2,1,0:T(8,128)(2,1)} %table_ref.1, bf16[64,8192]{1,0:T(8,128)(2,1)} %fields_ref.1, f32[5,128]{1,0:T(8,128)} %prior_ref.1), custom_call_target="tpu_custom_call" | custom-call | tf_op jit(solution)/shard_map/pallas_call | solution.py:333
  53.3 7.0 %shard_map.56 = f32[64,8192]{1,0:T(8,128)} custom-call(s32[64,128]{1,0:T(8,128)} %bitcast.2, f32[5,8192]{1,0:T(8,128)} %amp_ref.3, bf16[320,512]{1,0:T(8,128)(2,1)} %shard_map.55.f_ref), custom_call_target="tpu_custom_call" | custom-call | tf_op jit(solution)/shard_map/pallas_call | solution.py:353

commit v3 on v2

--- a/solution.py
+++ b/solution.py
@@ -79,7 +79,7 @@
     return hi, mid, rest - mid
 
 
-def inverse_factor(a, o_ref, m_ref, t_ref, tb_ref, q_ref):
+def inverse_factor(a, o_ref, m_ref, t_ref, tb_ref, q_ref, hook=None, hook_at=0):
     n = a.shape[0]
     sub, lane, lane2 = iota((PANEL, n), 0), iota((PANEL, n), 1), iota((n, n), 1)
     zero = jnp.zeros((PANEL, n), f32)
@@ -88,6 +88,8 @@
     q_ref[...] = jnp.zeros((n, n), bf16)
 
     def body(b, rows):
+        if hook is not None:
+            pl.when(b == hook_at)(hook)
         off = pl.multiple_of(b * PANEL, PANEL)
         prev = off - PANEL
         cols = [
@@ -129,12 +131,33 @@
     lax.fori_loop(0, n // PANEL, body, m_ref[0:PANEL, :])
 
 
+def pieces(v):
+    hi = v.astype(bf16)
+    rest = v - hi.astype(f32)
+    mid = rest.astype(bf16)
+    return hi, mid, (rest - mid.astype(f32)).astype(bf16)
+
+
+def product(a, b, axis):
+    ah, am, al = pieces(a)
+    bh, bm, bl = pieces(b)
+    left, right = jnp.concatenate([ah, am], axis=1), jnp.concatenate([ah, al], axis=1)
+    deep = lambda u, v: jnp.concatenate([u, v], axis=axis)
+    mul = lambda u, v: lax.dot_general(u, v, (((1,), (axis,)), ((), ())), preferred_element_type=f32)
+    n = b.shape[1 - axis]
+    small = mul(right, deep(bl, bh))
+    if n == 128:
+        both = mul(left, jnp.concatenate([deep(bh, bh), deep(bm, bm)], axis=1 - axis))
+        return both[:, :n] + (both[:, n:] + small)
+    return mul(left, deep(bh, bh)) + (mul(left, deep(bm, bm)) + small)
+
+
 def dot(a, b):
-    return jnp.dot(a, b, precision=highest, preferred_element_type=f32)
+    return product(a, b, 0)
 
 
 def dot_nt(a, b):
-    return lax.dot_general(a, b, (((1,), (1,)), ((), ())), precision=highest, preferred_element_type=f32)
+    return product(a, b, 1)
 
 
 def split2(v):
@@ -147,7 +170,7 @@
 
 
 def tree_kernel(pattern_ref, amp_ref, table_ref, fields_ref, prior_ref, out_ref,
-                acc_ref, cpart_ref, bt_ref, wall_ref, cpiece_ref, csum_ref, g_ref, linv_ref, x_ref, z_ref, m_ref, t_ref, tb_ref, q_ref,
+                acc_ref, cpart_ref, bt_ref, wall_ref, cpiece_ref, csum_ref, g_ref, linv_ref, x_ref, xt_ref, yt_ref, z_ref, m_ref, t_ref, tb_ref, q_ref,
                 s4, s4r, c4, c4r, s3, s3r, c3, c3r, s2, s2r, c2, c2r, s1, s1r, c1, c1r, send_sem, recv_sem):
     tiers, patterns, knots = table_ref.shape
     nf = fields_ref.shape[0]
@@ -171,12 +194,16 @@
     z_peers = [flip(8), flip(8, 16), flip(16)]
     started = []
 
-    def send(src, dst, k, dev):
+    def make(src, dst, k, dev):
         copy = pltpu.make_async_remote_copy(
             src_ref=src, dst_ref=dst, send_sem=send_sem.at[k], recv_sem=recv_sem.at[k],
             device_id=dev, device_id_type=pl.DeviceIdType.MESH)
+        started.append(copy)
+        return copy
+
+    def send(src, dst, k, dev):
+        copy = make(src, dst, k, dev)
         copy.start()
-        started.append(copy)
         return copy
 
     barrier = pltpu.get_barrier_semaphore()
@@ -217,68 +244,45 @@
     ]
 
     eye = iota((knots, knots), 0) == iota((knots, knots), 1)
-
-    def factor(t, block):
-        inverse_factor(block + jnp.where(eye, prior_ref[t:t + 1, :], 0.0), linv_ref.at[t], m_ref, t_ref, tb_ref, q_ref)
-
-    def eliminate(t, g, c, sem, before_rest, before_c):
-        factor(t, g(t, t))
-        linv = linv_ref[t]
+    core = lax.rem(region, 2)
+    half = pl.ds(pl.multiple_of(core * (knots // 2), knots // 2), knots // 2)
+
+    def factor(t, block, hook=None, hook_at=0):
+        inverse_factor(block + jnp.where(eye, prior_ref[t:t + 1, :], 0.0), linv_ref.at[t],
+                       m_ref, t_ref, tb_ref, q_ref, hook, hook_at)
+
+    def first_block(t, g):
         last = t - 1
-        before_rest()
-        xl = dot(linv, g(t, last))
-        x_ref[tri(t - 1, last)] = xl
-        own[t][tri(last, last)] = g(last, last) - dot(xl.T, xl)
-        copies = []
-        n_tri = tri(last, last)
-        devs = z_peers if t == 1 else [tree_peer[t]]
-        for k, dev in enumerate(devs):
-            dst = got[t].at[k] if t == 1 else got[t].at[n_tri]
-            copies.append(send(own[t].at[n_tri], dst, sem + k, dev))
-        xs = [xl]
-        if last:
-            rest = dot(linv, jnp.concatenate([g(t, s) for s in range(last)], axis=1))
-            xs = [rest[:, s * knots:(s + 1) * knots] for s in range(last)] + [xl]
-            for s in range(last):
-                x_ref[tri(t - 1, s)] = xs[s]
-            for u in range(last, -1, -1):
-                width = min(u + 1, last)
-                prod = dot(xs[u].T, rest[:, :width * knots])
-                for s in range(width):
-                    own[t][tri(u, s)] = g(u, s) - prod[:, s * knots:(s + 1) * knots]
-            for src, dst, k, dev in rest_parts(t, n_tri, sem):
-                copies.append(send(src, dst, k, dev))
-        before_c()
-        z = dot_nt(c(t), linv)
+        xl = dot(linv_ref[t], g(t, last))
+        x_ref[tri(last, last)] = xl
+        xt_ref[tri(last, last)] = xl.T
+        own[t][tri(last, last)] = g(last, last) - dot(xt_ref[tri(last, last)], xl)
+
+    def other_blocks(t, g):
+        last = t - 1
+        rest = dot(linv_ref[t], jnp.concatenate([g(t, s) for s in range(last)], axis=1))
+        for s in range(last):
+            xs = rest[:, s * knots:(s + 1) * knots]
+            x_ref[tri(last, s)] = xs
+            xt_ref[tri(last, s)] = xs.T
+        for u in range(last, -1, -1):
+            width = min(u + 1, last)
+            prod = dot(xt_ref[tri(last, u)], rest[:, :width * knots])
+            for s in range(width):
+                own[t][tri(u, s)] = g(u, s) - prod[:, s * knots:(s + 1) * knots]
+
+    def projections(t, c):
+        z = dot_nt(c(t), linv_ref[t])
         z_ref[t] = z
-        red = dot(z, jnp.concatenate(xs, axis=1))
+        red = dot(z, jnp.concatenate([x_ref[tri(t - 1, s)] for s in range(t)], axis=1))
         for s in range(t):
             cown[t][s] = c(s) - red[:, s * knots:(s + 1) * knots]
-        if t == 1:
-            for k, dev in enumerate(devs):
-                copies.append(send(cown[t].at[0], cgot[t].at[k], sem + 3 + k, dev))
-        elif t == 3:
-            part = pl.ds(pl.multiple_of(core * (nf // 2), nf // 2), nf // 2)
-            copies.append(send(cown[t].at[:, part, :], cgot[t].at[:, part, :], sem + 2, devs[0]))
-        else:
-            copies.append(send(cown[t], cgot[t], sem + 2, devs[0]))
-        return copies
-
-    core = lax.rem(region, 2)
-    half = pl.ds(pl.multiple_of(core * (knots // 2), knots // 2), knots // 2)
-
-    def rest_parts(t, n_tri, sem):
-        if t == 3:
-            return [(own[t].at[pl.ds(0, n_tri), half, :], got[t].at[pl.ds(0, n_tri), half, :], sem + 1, tree_peer[t])]
-        return [(own[t].at[pl.ds(0, n_tri)], got[t].at[pl.ds(0, n_tri)], sem + 1, tree_peer[t])]
-
-    nothing = lambda: None
-
-    def wait_ag():
-        for copy in ag_copies:
-            copy.wait_recv()
-
-    e4 = eliminate(4, lambda t, s: g_ref[tri(t, s)], lambda s: csum_ref[s], 9, nothing, wait_ag)
+
+    def prepare_descent(t):
+        y = dot(jnp.concatenate([xt_ref[tri(t - 1, s)] for s in range(t)], axis=0), linv_ref[t])
+        for s in range(t):
+            yt_ref[tri(t - 1, s)] = y[s * knots:(s + 1) * knots]
+        z_ref[t] = dot(z_ref[t], linv_ref[t])
 
     def summed(t):
         return lambda u, s: own[t][tri(u, s)] + got[t][tri(u, s)]
@@ -286,36 +290,80 @@
     def csummed(t):
         return lambda s: cown[t][s] + cgot[t][s]
 
-    e4[0].wait_recv()
-    e3 = eliminate(3, summed(4), csummed(4), 12, e4[1].wait_recv, e4[2].wait_recv)
-    e3[0].wait_recv()
-    relays = []
-
-    def relay_rest():
-        e3[1].wait_recv()
-        part = got[3].at[pl.ds(0, 5), half, :]
-        relays.append(send(part, part, 15, tree_peer[4]))
-        e3[2].wait_recv()
-        fields = pl.ds(pl.multiple_of(core * (nf // 2), nf // 2), nf // 2)
-        part = cgot[3].at[:, fields, :]
-        relays.append(send(part, part, 16, tree_peer[4]))
-        relays[0].wait_recv()
-
-    e2 = eliminate(2, summed(3), csummed(3), 17, relay_rest, lambda: relays[1].wait_recv())
-    e2[0].wait_recv()
-    e1 = eliminate(1, summed(2), csummed(2), 20, e2[1].wait_recv, e2[2].wait_recv)
-    for copy in e1[:3]:
+    g4 = lambda t, s: g_ref[tri(t, s)]
+    sibling, across, beyond = tree_peer[4], tree_peer[3], tree_peer[2]
+
+    factor(4, g4(4, 4))
+    first_block(4, g4)
+    a4 = send(s4.at[9], s4r.at[9], 9, sibling)
+    other_blocks(4, g4)
+    b4 = send(s4.at[pl.ds(0, 9)], s4r.at[pl.ds(0, 9)], 10, sibling)
+    a4.wait_recv()
+
+    g3 = summed(4)
+    factor(3, g3(3, 3))
+    b4.wait_recv()
+    first_block(3, g3)
+    a3 = send(s3.at[5], s3r.at[5], 12, across)
+    other_blocks(3, g3)
+    near, far = pl.ds(2, 3), pl.ds(0, 2)
+    b3 = send(s3.at[near, half, :], s3r.at[near, half, :], 13, across)
+    d3 = send(s3.at[far, half, :], s3r.at[far, half, :], 14, across)
+    for copy in ag_copies:
         copy.wait_recv()
-    factor(0, (own[1][0] + got[1][0]) + (got[1][1] + got[1][2]))
-    linv = linv_ref[0]
-    for copy in e1[3:]:
+    projections(4, lambda s: csum_ref[s])
+    e4 = send(c4, c4r, 11, sibling)
+    a3.wait_recv()
+
+    g2 = summed(3)
+    relay_near = make(s3r.at[near, half, :], s3r.at[near, half, :], 16, sibling)
+
+    def hand_over():
+        b3.wait_recv()
+        relay_near.start()
+
+    factor(2, g2(2, 2), hand_over, 5)
+    relay_near.wait_recv()
+    first_block(2, g2)
+    a2 = send(s2.at[2], s2r.at[2], 18, beyond)
+    d3.wait_recv()
+    relay_far = send(s3r.at[far, half, :], s3r.at[far, half, :], 17, sibling)
+    e4.wait_recv()
+    projections(3, csummed(4))
+    e3 = send(c3, c3r, 15, across)
+    relay_far.wait_recv()
+    other_blocks(2, g2)
+    b2 = send(s2.at[pl.ds(0, 2)], s2r.at[pl.ds(0, 2)], 19, beyond)
+    a2.wait_recv()
+
+    g1 = summed(2)
+    factor(1, g1(1, 1))
+    b2.wait_recv()
+    first_block(1, g1)
+    a1 = [send(s1.at[0], s1r.at[k], 21 + k, dev) for k, dev in enumerate(z_peers)]
+    e3.wait_recv()
+    projections(2, csummed(3))
+    e2 = send(c2, c2r, 20, beyond)
+    prepare_descent(4)
+    prepare_descent(3)
+    e2.wait_recv()
+    projections(1, csummed(2))
+    e1 = [send(c1.at[0], c1r.at[k], 24 + k, dev) for k, dev in enumerate(z_peers)]
+    prepare_descent(2)
+    prepare_descent(1)
+    for copy in a1:
         copy.wait_recv()
-    c0 = (cown[1][0] + cgot[1][0]) + (cgot[1][1] + cgot[1][2])
-    wts = [dot(dot_nt(c0, linv), linv)]
-    for t in range(1, tiers):
-        x = jnp.concatenate([x_ref[tri(t - 1, s)] for s in range(t)], axis=1)
-        target = z_ref[t] - dot_nt(jnp.concatenate(wts, axis=1), x)
-        wts.append(dot(target, linv_ref[t]))
+    factor(0, (s1[0] + s1r[0]) + (s1r[1] + s1r[2]))
+    for copy in e1:
+        copy.wait_recv()
+    c0 = (c1[0] + c1r[0]) + (c1r[1] + c1r[2])
+    wts = [dot(dot_nt(c0, linv_ref[0]), linv_ref[0])]
+    left = {t: z_ref[t] for t in range(1, tiers)}
+    for s in range(top):
+        moved = dot(wts[s], jnp.concatenate([yt_ref[tri(t - 1, s)] for t in range(s + 1, tiers)], axis=1))
+        for t in range(s + 1, tiers):
+            left[t] = left[t] - moved[:, (t - s - 1) * knots:(t - s) * knots]
+        wts.append(left[s + 1])
     for t in range(tiers):
         both = jnp.dot(split2(wts[t]), bt_ref[t], preferred_element_type=f32)
         out_ref[t * nf:(t + 1) * nf, :] = (both[:nf] + both[nf:]).astype(bf16)
@@ -338,14 +386,14 @@
             pltpu.VMEM((tiers, knots, patterns), bf16),
             pltpu.VMEM((4, 16, patterns), f32),
             pltpu.VMEM((3, tiers, nf // 4, knots), f32),
-            rhs(tiers), block(15), block(5), block(10), rhs(5),
+            rhs(tiers), block(15), block(5), block(10), block(10), block(10), rhs(5),
             pltpu.VMEM((knots, knots), f32), pltpu.VMEM((knots, knots), f32),
             pltpu.VMEM((knots, knots), bf16), pltpu.VMEM((knots, knots), bf16),
             block(10), block(10), rhs(4), rhs(4),
             block(6), block(6), rhs(3), rhs(3),
             block(3), block(3), rhs(2), rhs(2),
             block(1), block(3), rhs(1), rhs(3),
-            pltpu.SemaphoreType.DMA((26,)), pltpu.SemaphoreType.DMA((26,)),
+            pltpu.SemaphoreType.DMA((27,)), pltpu.SemaphoreType.DMA((27,)),
         ],
         compiler_params=pltpu.CompilerParams(collective_id=0, has_side_effects=True),
     )(pattern2, amplitude, basis_table, fields, prior_precision)

time: 61.4 us -> 57.1 us (0.930)
  Pallas kernels: 60.4 us -> 56.4 us
    pallas_call x1, Pallas kernels: 53.3 us -> 49.4 us  [shards(): pl.pallas_call(tree_kernel, out_shape=jax.ShapeDtypeStruct((tiers * nf, p...]
where the time goes in v3:
time: 57.1 us; the launch traced here: 56.4 us
  Pallas kernels  56.4 us (99%)
    pallas_call x1, Pallas kernels, shards(): pl.pallas_call(tree_kernel, out_shape=jax.ShapeDtypeStruct((tiers * nf, p...  49.4 us
    pallas_call x1, Pallas kernels, shards(): pl.pallas_call(fit_kernel, grid=(obs // chunk,), in_specs=[pl.BlockSpec((...  7.04 us

profile of v3, /device:TPU:0, one launch (start us, length us, event | category | flops | bytes accessed | tf_op | source)
XLA Modules:
  0.0 56.4 jit_solution(5239982666095686680)
XLA Ops:
  0.0 49.4 %shard_map.55.f_ref = bf16[320,512]{1,0:T(8,128)(2,1)} custom-call(s32[64,128]{1,0:T(8,128)} %bitcast.1, f32[5,8192]{1,0:T(8,128)} %amp_ref.3, bf16[5,512,128]{2,1,0:T(8,128)(2,1)} %table_ref.1, bf16[64,8192]{1,0:T(8,128)(2,1)} %fields_ref.1, f32[5,128]{1,0:T(8,128)} %prior_ref.1), custom_call_target="tpu_custom_call" | custom-call | tf_op jit(solution)/shard_map/pallas_call | solution.py:381
  49.4 7.0 %shard_map.56 = f32[64,8192]{1,0:T(8,128)} custom-call(s32[64,128]{1,0:T(8,128)} %bitcast.2, f32[5,8192]{1,0:T(8,128)} %amp_ref.3, bf16[320,512]{1,0:T(8,128)(2,1)} %shard_map.55.f_ref), custom_call_target="tpu_custom_call" | custom-call | tf_op jit(solution)/shard_map/pallas_call | solution.py:401

commit v4 on v3

--- a/solution.py
+++ b/solution.py
@@ -40,20 +40,12 @@
     return jnp.concatenate(parts, axis=1)
 
 
-def accumulate(pattern_ref, amp_ref, fields_ref, acc_ref, chunk):
-    tiers, obs = amp_ref.shape
+def accumulate(pattern_ref, acc_ref, obs, chunk, lhs_of):
     patterns = acc_ref.shape[1]
     acc_ref[...] = jnp.zeros_like(acc_ref)
 
     def step(i, carry):
-        off = pl.multiple_of(i * chunk, chunk)
-        amp = amp_ref[:, pl.ds(off, chunk)]
-        fields = fields_ref[:, pl.ds(off, chunk)].astype(f32)
-        prod = amplitude_products(amp)
-        hi = prod.astype(bf16)
-        lo = (prod - hi.astype(f32)).astype(bf16)
-        rows = [(fields * amp[t:t + 1, :]).astype(bf16) for t in range(tiers)]
-        lhs = jnp.concatenate(rows + [hi, lo], axis=0)
+        lhs = lhs_of(pl.ds(pl.multiple_of(i * chunk, chunk), chunk))
         hot = one_hot(pattern_ref, i * (chunk // 128), chunk // 128, patterns)
         acc_ref[...] += lax.dot_general(lhs, hot, (((1,), (1,)), ((), ())), preferred_element_type=f32)
         return carry
@@ -64,12 +56,15 @@
 def fit_kernel(pattern_ref, amp_ref, f_ref, out_ref):
     tiers = amp_ref.shape[0]
     nf, chunk = out_ref.shape
-    hot = one_hot(pattern_ref, 0, chunk // 128, f_ref.shape[1])
-    part = jnp.dot(f_ref[...], hot, preferred_element_type=f32)
-    total = part[:nf] * amp_ref[0:1, :]
-    for t in range(1, tiers):
-        total = total + part[t * nf:(t + 1) * nf] * amp_ref[t:t + 1, :]
-    out_ref[...] = total
+    part_of = min(1024, chunk)
+    for first in range(0, chunk, part_of):
+        cut = slice(first, first + part_of)
+        hot = one_hot(pattern_ref, first // 128, part_of // 128, f_ref.shape[1])
+        part = jnp.dot(f_ref[...], hot, preferred_element_type=f32)
+        total = part[:nf] * amp_ref[0:1, cut]
+        for t in range(1, tiers):
+            total = total + part[t * nf:(t + 1) * nf] * amp_ref[t:t + 1, cut]
+        out_ref[:, cut] = total
 
 
 def split3(v):
@@ -170,8 +165,8 @@
 
 
 def tree_kernel(pattern_ref, amp_ref, table_ref, fields_ref, prior_ref, out_ref,
-                acc_ref, cpart_ref, bt_ref, wall_ref, cpiece_ref, csum_ref, g_ref, linv_ref, x_ref, xt_ref, yt_ref, z_ref, m_ref, t_ref, tb_ref, q_ref,
-                s4, s4r, c4, c4r, s3, s3r, c3, c3r, s2, s2r, c2, c2r, s1, s1r, c1, c1r, send_sem, recv_sem):
+                accw_ref, acc_ref, cpart_ref, bt_ref, wall_ref, cpiece_ref, csum_ref, g_ref, linv_ref, x_ref, xt_ref, yt_ref, z_ref, m_ref, t_ref, tb_ref, q_ref,
+                s4, s4r, c4, c4r, s3, s3r, c3, c3r, s2, s2r, c2, c2r, s1, s1r, c1, c1r, root_ref, send_sem, recv_sem):
     tiers, patterns, knots = table_ref.shape
     nf = fields_ref.shape[0]
     top = tiers - 1
@@ -210,12 +205,23 @@
     peers = y_peers + list(tree_peer.values()) + z_peers
     for dev in peers:
         pl.semaphore_signal(barrier, inc=1, device_id=dev, device_id_type=pl.DeviceIdType.MESH)
-    accumulate(pattern_ref, amp_ref, fields_ref, acc_ref, 1024)
-    base = tiers * nf
-    wall_ref[obs] = acc_ref[base:base + 16, :] + acc_ref[base + 16:base + 32, :]
+    def amplitude_rows(cut):
+        prod = amplitude_products(amp_ref[:, cut])
+        hi = prod.astype(bf16)
+        return jnp.concatenate([hi, (prod - hi.astype(f32)).astype(bf16)], axis=0)
+
+    def field_rows(cut):
+        amp = amp_ref[:, cut]
+        fields = fields_ref[:, cut].astype(f32)
+        return jnp.concatenate([(fields * amp[t:t + 1, :]).astype(bf16) for t in range(tiers)], axis=0)
+
+    n_here = amp_ref.shape[1]
+    accumulate(pattern_ref, accw_ref, n_here, 1024, amplitude_rows)
+    wall_ref[obs] = accw_ref[0:16, :] + accw_ref[16:32, :]
     pl.semaphore_wait(barrier, len(peers))
 
     w_copies = [send(wall_ref.at[obs], wall_ref.at[obs], k, dev) for k, dev in enumerate(y_peers)]
+    accumulate(pattern_ref, acc_ref, n_here, 1024, field_rows)
     for t in range(tiers):
         v = split2(acc_ref[t * nf:(t + 1) * nf, :])
         both = jnp.dot(v, table_ref[t], preferred_element_type=f32)
@@ -340,7 +346,7 @@
     factor(1, g1(1, 1))
     b2.wait_recv()
     first_block(1, g1)
-    a1 = [send(s1.at[0], s1r.at[k], 21 + k, dev) for k, dev in enumerate(z_peers)]
+    a1 = [send(s1.at[0, half, :], s1r.at[k, half, :], 21 + k, dev) for k, dev in enumerate(z_peers)]
     e3.wait_recv()
     projections(2, csummed(3))
     e2 = send(c2, c2r, 20, beyond)
@@ -353,7 +359,10 @@
     prepare_descent(1)
     for copy in a1:
         copy.wait_recv()
-    factor(0, (s1[0] + s1r[0]) + (s1r[1] + s1r[2]))
+    root_ref[half, :] = (s1[0, half, :] + s1r[0, half, :]) + (s1r[1, half, :] + s1r[2, half, :])
+    whole = send(root_ref.at[half, :], root_ref.at[half, :], 27, sibling)
+    whole.wait_recv()
+    factor(0, root_ref[...])
     for copy in e1:
         copy.wait_recv()
     c0 = (c1[0] + c1r[0]) + (c1r[1] + c1r[2])
@@ -382,7 +391,7 @@
         tree_kernel,
         out_shape=jax.ShapeDtypeStruct((tiers * nf, patterns), bf16),
         scratch_shapes=[
-            pltpu.VMEM((tiers * nf + 32, patterns), f32), rhs(tiers),
+            pltpu.VMEM((32, patterns), f32), pltpu.VMEM((tiers * nf, patterns), f32), rhs(tiers),
             pltpu.VMEM((tiers, knots, patterns), bf16),
             pltpu.VMEM((4, 16, patterns), f32),
             pltpu.VMEM((3, tiers, nf // 4, knots), f32),
@@ -392,12 +401,12 @@
             block(10), block(10), rhs(4), rhs(4),
             block(6), block(6), rhs(3), rhs(3),
             block(3), block(3), rhs(2), rhs(2),
-            block(1), block(3), rhs(1), rhs(3),
-            pltpu.SemaphoreType.DMA((27,)), pltpu.SemaphoreType.DMA((27,)),
+            block(1), block(3), rhs(1), rhs(3), pltpu.VMEM((knots, knots), f32),
+            pltpu.SemaphoreType.DMA((28,)), pltpu.SemaphoreType.DMA((28,)),
         ],
         compiler_params=pltpu.CompilerParams(collective_id=0, has_side_effects=True),
     )(pattern2, amplitude, basis_table, fields, prior_precision)
-    chunk = min(1024, obs)
+    chunk = min(2048, obs)
     return pl.pallas_call(
         fit_kernel,
         grid=(obs // chunk,),

time: 57.1 us -> 57.7 us (1.011)
    pallas_call x1, Pallas kernels: 49.4 us -> 51.1 us  [shards(): pl.pallas_call(tree_kernel, out_shape=jax.ShapeDtypeStruct((tiers * nf, p...]
    pallas_call x1, Pallas kernels: 7.04 us -> 5.7 us  [shards(): pl.pallas_call(fit_kernel, grid=(obs // chunk,), in_specs=[pl.BlockSpec((...]
where the time goes in v4:
time: 57.7 us; the launch traced here: 56.9 us
  Pallas kernels  56.8 us (98%)
    pallas_call x1, Pallas kernels, shards(): pl.pallas_call(tree_kernel, out_shape=jax.ShapeDtypeStruct((tiers * nf, p...  51.1 us
    pallas_call x1, Pallas kernels, shards(): pl.pallas_call(fit_kernel, grid=(obs // chunk,), in_specs=[pl.BlockSpec((...  5.7 us

profile of v4, /device:TPU:0, one launch (start us, length us, event | category | flops | bytes accessed | tf_op | source)
XLA Modules:
  0.0 56.9 jit_solution(2629975763554513582)
XLA Ops:
  0.0 51.1 %shard_map.55.f_ref = bf16[320,512]{1,0:T(8,128)(2,1)} custom-call(s32[64,128]{1,0:T(8,128)} %bitcast.1, f32[5,8192]{1,0:T(8,128)} %amp_ref.3, bf16[5,512,128]{2,1,0:T(8,128)(2,1)} %table_ref.1, bf16[64,8192]{1,0:T(8,128)(2,1)} %fields_ref.1, f32[5,128]{1,0:T(8,128)} %prior_ref.1), custom_call_target="tpu_custom_call" | custom-call | tf_op jit(solution)/shard_map/pallas_call | solution.py:390
  51.2 5.7 %shard_map.56 = f32[64,8192]{1,0:T(8,128)} custom-call(s32[64,128]{1,0:T(8,128)} %bitcast.2, f32[5,8192]{1,0:T(8,128)} %amp_ref.3, bf16[320,512]{1,0:T(8,128)(2,1)} %shard_map.55.f_ref), custom_call_target="tpu_custom_call" | custom-call | tf_op jit(solution)/shard_map/pallas_call | solution.py:410

commit v5 on v4

--- a/solution.py
+++ b/solution.py
@@ -31,22 +31,31 @@
     return jnp.concatenate([l0 * r0, l1 * r1], axis=0)
 
 
-def one_hot(pattern_ref, first_row, rows, patterns):
-    parts = []
+def one_hot(pattern_ref, first_row, rows, patterns, fold=None):
+    parts, masks = [], []
     ids = iota((patterns, 128), 0)
     for r in range(rows):
         row = pattern_ref[pl.ds(first_row + r, 1), :]
+        if fold is not None:
+            below = row < fold
+            masks.append(jnp.where(below, 1.0, 0.0))
+            row = jnp.where(below, row, row - fold)
         parts.append((jnp.broadcast_to(row, (patterns, 128)) == ids).astype(f32).astype(bf16))
-    return jnp.concatenate(parts, axis=1)
-
-
-def accumulate(pattern_ref, acc_ref, obs, chunk, lhs_of):
+    hot = jnp.concatenate(parts, axis=1)
+    return hot if fold is None else (hot, jnp.concatenate(masks, axis=1))
+
+
+def accumulate(pattern_ref, acc_ref, obs, chunk, lhs_of, fold=None):
     patterns = acc_ref.shape[1]
     acc_ref[...] = jnp.zeros_like(acc_ref)
 
     def step(i, carry):
         lhs = lhs_of(pl.ds(pl.multiple_of(i * chunk, chunk), chunk))
-        hot = one_hot(pattern_ref, i * (chunk // 128), chunk // 128, patterns)
+        hot = one_hot(pattern_ref, i * (chunk // 128), chunk // 128, patterns, fold)
+        if fold is not None:
+            hot, below = hot
+            first = lhs * below.astype(bf16)
+            lhs = jnp.concatenate([first, lhs - first], axis=0)
         acc_ref[...] += lax.dot_general(lhs, hot, (((1,), (1,)), ((), ())), preferred_element_type=f32)
         return carry
 
@@ -164,9 +173,9 @@
     return t * (t + 1) // 2 + s
 
 
-def tree_kernel(pattern_ref, amp_ref, table_ref, fields_ref, prior_ref, out_ref,
-                accw_ref, acc_ref, cpart_ref, bt_ref, wall_ref, cpiece_ref, csum_ref, g_ref, linv_ref, x_ref, xt_ref, yt_ref, z_ref, m_ref, t_ref, tb_ref, q_ref,
-                s4, s4r, c4, c4r, s3, s3r, c3, c3r, s2, s2r, c2, c2r, s1, s1r, c1, c1r, root_ref, send_sem, recv_sem):
+def tree_kernel(pattern_ref, amp_ref, table_any, fields_any, prior_ref, out_ref,
+                table_ref, fields_ref, load_sem, accw_ref, acc_ref, cpart_ref, bt_ref, wall_ref, cpiece_ref, csum_ref, g_ref, linv_ref, x_ref, xt_ref, yt_ref, z_ref, m_ref, t_ref, tb_ref, q_ref,
+                s4, s4r, c4, c4r, s3, s3r, c3, c3r, s2, s2r, c2, c2r, s1, s1r, c1, c1r, send_sem, recv_sem):
     tiers, patterns, knots = table_ref.shape
     nf = fields_ref.shape[0]
     top = tiers - 1
@@ -205,6 +214,11 @@
     peers = y_peers + list(tree_peer.values()) + z_peers
     for dev in peers:
         pl.semaphore_signal(barrier, inc=1, device_id=dev, device_id_type=pl.DeviceIdType.MESH)
+    loads = [pltpu.make_async_copy(fields_any, fields_ref, load_sem.at[0]),
+             pltpu.make_async_copy(table_any, table_ref, load_sem.at[1])]
+    for load in loads:
+        load.start()
+
     def amplitude_rows(cut):
         prod = amplitude_products(amp_ref[:, cut])
         hi = prod.astype(bf16)
@@ -216,12 +230,16 @@
         return jnp.concatenate([(fields * amp[t:t + 1, :]).astype(bf16) for t in range(tiers)], axis=0)
 
     n_here = amp_ref.shape[1]
-    accumulate(pattern_ref, accw_ref, n_here, 1024, amplitude_rows)
-    wall_ref[obs] = accw_ref[0:16, :] + accw_ref[16:32, :]
+    fold = patterns // 2
+    accumulate(pattern_ref, accw_ref, n_here, 4096, amplitude_rows, fold)
+    wall_ref[obs, :, 0:fold] = accw_ref[0:16, :] + accw_ref[16:32, :]
+    wall_ref[obs, :, fold:patterns] = accw_ref[32:48, :] + accw_ref[48:64, :]
     pl.semaphore_wait(barrier, len(peers))
 
     w_copies = [send(wall_ref.at[obs], wall_ref.at[obs], k, dev) for k, dev in enumerate(y_peers)]
-    accumulate(pattern_ref, acc_ref, n_here, 1024, field_rows)
+    for load in loads:
+        load.wait()
+    accumulate(pattern_ref, acc_ref, n_here, 2048, field_rows)
     for t in range(tiers):
         v = split2(acc_ref[t * nf:(t + 1) * nf, :])
         both = jnp.dot(v, table_ref[t], preferred_element_type=f32)
@@ -346,7 +364,7 @@
     factor(1, g1(1, 1))
     b2.wait_recv()
     first_block(1, g1)
-    a1 = [send(s1.at[0, half, :], s1r.at[k, half, :], 21 + k, dev) for k, dev in enumerate(z_peers)]
+    a1 = [send(s1.at[0], s1r.at[k], 21 + k, dev) for k, dev in enumerate(z_peers)]
     e3.wait_recv()
     projections(2, csummed(3))
     e2 = send(c2, c2r, 20, beyond)
@@ -359,10 +377,7 @@
     prepare_descent(1)
     for copy in a1:
         copy.wait_recv()
-    root_ref[half, :] = (s1[0, half, :] + s1r[0, half, :]) + (s1r[1, half, :] + s1r[2, half, :])
-    whole = send(root_ref.at[half, :], root_ref.at[half, :], 27, sibling)
-    whole.wait_recv()
-    factor(0, root_ref[...])
+    factor(0, (s1[0] + s1r[0]) + (s1r[1] + s1r[2]))
     for copy in e1:
         copy.wait_recv()
     c0 = (c1[0] + c1r[0]) + (c1r[1] + c1r[2])
@@ -390,8 +405,14 @@
     per_pattern = pl.pallas_call(
         tree_kernel,
         out_shape=jax.ShapeDtypeStruct((tiers * nf, patterns), bf16),
+        in_specs=[
+            pl.BlockSpec(memory_space=pltpu.VMEM), pl.BlockSpec(memory_space=pltpu.VMEM),
+            pl.BlockSpec(memory_space=pl.ANY), pl.BlockSpec(memory_space=pl.ANY),
+            pl.BlockSpec(memory_space=pltpu.VMEM),
+        ],
         scratch_shapes=[
-            pltpu.VMEM((32, patterns), f32), pltpu.VMEM((tiers * nf, patterns), f32), rhs(tiers),
+            pltpu.VMEM(basis_table.shape, bf16), pltpu.VMEM(fields.shape, bf16), pltpu.SemaphoreType.DMA((2,)),
+            pltpu.VMEM((64, patterns // 2), f32), pltpu.VMEM((tiers * nf, patterns), f32), rhs(tiers),
             pltpu.VMEM((tiers, knots, patterns), bf16),
             pltpu.VMEM((4, 16, patterns), f32),
             pltpu.VMEM((3, tiers, nf // 4, knots), f32),
@@ -401,8 +422,8 @@
             block(10), block(10), rhs(4), rhs(4),
             block(6), block(6), rhs(3), rhs(3),
             block(3), block(3), rhs(2), rhs(2),
-            block(1), block(3), rhs(1), rhs(3), pltpu.VMEM((knots, knots), f32),
-            pltpu.SemaphoreType.DMA((28,)), pltpu.SemaphoreType.DMA((28,)),
+            block(1), block(3), rhs(1), rhs(3),
+            pltpu.SemaphoreType.DMA((27,)), pltpu.SemaphoreType.DMA((27,)),
         ],
         compiler_params=pltpu.CompilerParams(collective_id=0, has_side_effects=True),
     )(pattern2, amplitude, basis_table, fields, prior_precision)

time: 57.7 us -> 53.9 us (0.934); the launches traced: 56.9 us -> 53.6 us
  Pallas kernels: 56.8 us -> 53.6 us
    pallas_call x1, Pallas kernels: 51.1 us -> 47.9 us  [shards(): pl.pallas_call(tree_kernel, out_shape=jax.ShapeDtypeStruct((tiers * nf, p...]
where the time goes in v5:
time: 53.9 us; the launch traced here: 53.6 us
  Pallas kernels  53.6 us (99%)
    pallas_call x1, Pallas kernels, shards(): pl.pallas_call(tree_kernel, out_shape=jax.ShapeDtypeStruct((tiers * nf, p...  47.9 us
    pallas_call x1, Pallas kernels, shards(): pl.pallas_call(fit_kernel, grid=(obs // chunk,), in_specs=[pl.BlockSpec((...  5.7 us

profile of v5, /device:TPU:0, one launch (start us, length us, event | category | flops | bytes accessed | tf_op | source)
XLA Modules:
  0.0 53.6 jit_solution(3093263082243045506)
XLA Ops:
  0.0 47.9 %shard_map.55.f_ref = bf16[320,512]{1,0:T(8,128)(2,1)} custom-call(s32[64,128]{1,0:T(8,128)} %bitcast.1, f32[5,8192]{1,0:T(8,128)} %amp_ref.3, bf16[5,512,128]{2,1,0:T(8,128)(2,1)} %table_any.1, bf16[64,8192]{1,0:T(8,128)(2,1)} %fields_any.1, f32[5,128]{1,0:T(8,128)} %prior_ref.1), custom_call_target="tpu_custom_call" | custom-call | tf_op jit(solution)/shard_map/pallas_call | solution.py:405
  47.9 5.7 %shard_map.56 = f32[64,8192]{1,0:T(8,128)} custom-call(s32[64,128]{1,0:T(8,128)} %bitcast.2, f32[5,8192]{1,0:T(8,128)} %amp_ref.3, bf16[320,512]{1,0:T(8,128)(2,1)} %shard_map.55.f_ref), custom_call_target="tpu_custom_call" | custom-call | tf_op jit(solution)/shard_map/pallas_call | solution.py:431

commit v6 on v5

--- a/solution.py
+++ b/solution.py
@@ -253,20 +253,16 @@
     for copy in w_copies:
         copy.wait_recv()
     w = (wall_ref[0] + wall_ref[1]) + (wall_ref[2] + wall_ref[3])
-    for t in range(top, -1, -1):
-        for s in range(t, -1, -1):
-            row = PAIR_ROW[(s, t)]
-            scaled = bt_ref[t].astype(f32) * w[row:row + 1, :]
-            both = lax.dot_general(split2(scaled), bt_ref[s], (((1,), (1,)), ((), ())), preferred_element_type=f32)
-            g_ref[tri(t, s)] = both[:knots] + both[knots:]
-    for copy in rs_copies:
-        copy.wait_recv()
-    mine = pl.ds(pl.multiple_of(obs * quarter, quarter), quarter)
-    csum_ref[:, mine, :] = cpart_ref[:, mine, :] + cpiece_ref[0] + cpiece_ref[1] + cpiece_ref[2]
-    ag_copies = [
-        send(csum_ref.at[:, mine, :], csum_ref.at[:, mine, :], 6 + k, dev) for k, dev in enumerate(y_peers)
-    ]
-
+
+    def build(t, s):
+        row = PAIR_ROW[(s, t)]
+        scaled = bt_ref[t].astype(f32) * w[row:row + 1, :]
+        both = lax.dot_general(split2(scaled), bt_ref[s], (((1,), (1,)), ((), ())), preferred_element_type=f32)
+        g_ref[tri(t, s)] = both[:knots] + both[knots:]
+
+    urgent = [(4, 4), (4, 3), (3, 3)]
+    for t, s in urgent:
+        build(t, s)
     eye = iota((knots, knots), 0) == iota((knots, knots), 1)
     core = lax.rem(region, 2)
     half = pl.ds(pl.multiple_of(core * (knots // 2), knots // 2), knots // 2)
@@ -320,6 +316,17 @@
     factor(4, g4(4, 4))
     first_block(4, g4)
     a4 = send(s4.at[9], s4r.at[9], 9, sibling)
+    for copy in rs_copies:
+        copy.wait_recv()
+    mine = pl.ds(pl.multiple_of(obs * quarter, quarter), quarter)
+    csum_ref[:, mine, :] = cpart_ref[:, mine, :] + cpiece_ref[0] + cpiece_ref[1] + cpiece_ref[2]
+    ag_copies = [
+        send(csum_ref.at[:, mine, :], csum_ref.at[:, mine, :], 6 + k, dev) for k, dev in enumerate(y_peers)
+    ]
+    for t in range(top, -1, -1):
+        for s in range(t, -1, -1):
+            if (t, s) not in urgent:
+                build(t, s)
     other_blocks(4, g4)
     b4 = send(s4.at[pl.ds(0, 9)], s4r.at[pl.ds(0, 9)], 10, sibling)
     a4.wait_recv()

time: 53.9 us -> 51.2 us (0.950)
  Pallas kernels: 53.6 us -> 50.9 us
    pallas_call x1, Pallas kernels: 47.9 us -> 45.2 us  [shards(): pl.pallas_call(tree_kernel, out_shape=jax.ShapeDtypeStruct((tiers * nf, p...]
where the time goes in v6:
time: 51.2 us; the launch traced here: 50.9 us
  Pallas kernels  50.9 us (99%)
    pallas_call x1, Pallas kernels, shards(): pl.pallas_call(tree_kernel, out_shape=jax.ShapeDtypeStruct((tiers * nf, p...  45.2 us
    pallas_call x1, Pallas kernels, shards(): pl.pallas_call(fit_kernel, grid=(obs // chunk,), in_specs=[pl.BlockSpec((...  5.7 us

profile of v6, /device:TPU:0, one launch (start us, length us, event | category | flops | bytes accessed | tf_op | source)
XLA Modules:
  0.0 50.9 jit_solution(3184035303905454431)
XLA Ops:
  0.0 45.2 %shard_map.55.f_ref = bf16[320,512]{1,0:T(8,128)(2,1)} custom-call(s32[64,128]{1,0:T(8,128)} %bitcast.1, f32[5,8192]{1,0:T(8,128)} %amp_ref.3, bf16[5,512,128]{2,1,0:T(8,128)(2,1)} %table_any.1, bf16[64,8192]{1,0:T(8,128)(2,1)} %fields_any.1, f32[5,128]{1,0:T(8,128)} %prior_ref.1), custom_call_target="tpu_custom_call" | custom-call | tf_op jit(solution)/shard_map/pallas_call | solution.py:412
  45.2 5.7 %shard_map.56 = f32[64,8192]{1,0:T(8,128)} custom-call(s32[64,128]{1,0:T(8,128)} %bitcast.2, f32[5,8192]{1,0:T(8,128)} %amp_ref.3, bf16[320,512]{1,0:T(8,128)(2,1)} %shard_map.55.f_ref), custom_call_target="tpu_custom_call" | custom-call | tf_op jit(solution)/shard_map/pallas_call | solution.py:438

commit v7 on v6

--- a/solution.py
+++ b/solution.py
@@ -186,7 +186,7 @@
     got = {4: s4r, 3: s3r, 2: s2r, 1: s1r}
     cown = {4: c4, 3: c3, 2: c2, 1: c1}
     cgot = {4: c4r, 3: c3r, 2: c2r, 1: c1r}
-    y_peers = [(region, lax.rem(obs + d, n_obs)) for d in range(1, n_obs)]
+    y_peers = [(region, lax.rem(obs + d, n_obs)) for d in (2, 1, 3)]
 
     def flip(*bits):
         other = region
@@ -195,7 +195,7 @@
         return other, obs
 
     tree_peer = {4: flip(1), 3: flip(2), 2: flip(2, 4)}
-    z_peers = [flip(8), flip(8, 16), flip(16)]
+    z_peers = [flip(16), flip(8), flip(8, 16)]
     started = []
 
     def make(src, dst, k, dev):
@@ -231,7 +231,7 @@
 
     n_here = amp_ref.shape[1]
     fold = patterns // 2
-    accumulate(pattern_ref, accw_ref, n_here, 4096, amplitude_rows, fold)
+    accumulate(pattern_ref, accw_ref, n_here, 8192, amplitude_rows, fold)
     wall_ref[obs, :, 0:fold] = accw_ref[0:16, :] + accw_ref[16:32, :]
     wall_ref[obs, :, fold:patterns] = accw_ref[32:48, :] + accw_ref[48:64, :]
     pl.semaphore_wait(barrier, len(peers))
@@ -384,10 +384,10 @@
     prepare_descent(1)
     for copy in a1:
         copy.wait_recv()
-    factor(0, (s1[0] + s1r[0]) + (s1r[1] + s1r[2]))
+    factor(0, (s1[0] + s1r[1]) + (s1r[2] + s1r[0]))
     for copy in e1:
         copy.wait_recv()
-    c0 = (c1[0] + c1r[0]) + (c1r[1] + c1r[2])
+    c0 = (c1[0] + c1r[1]) + (c1r[2] + c1r[0])
     wts = [dot(dot_nt(c0, linv_ref[0]), linv_ref[0])]
     left = {t: z_ref[t] for t in range(1, tiers)}
     for s in range(top):

time: 51.2 us -> 51 us (level)
  no operation moved by 1% of the time
where the time goes in v7:
time: 51 us; the launch traced here: 50.6 us
  Pallas kernels  50.6 us (99%)
    pallas_call x1, Pallas kernels, shards(): pl.pallas_call(tree_kernel, out_shape=jax.ShapeDtypeStruct((tiers * nf, p...  44.9 us
    pallas_call x1, Pallas kernels, shards(): pl.pallas_call(fit_kernel, grid=(obs // chunk,), in_specs=[pl.BlockSpec((...  5.7 us

profile of v7, /device:TPU:0, one launch (start us, length us, event | category | flops | bytes accessed | tf_op | source)
XLA Modules:
  0.0 50.6 jit_solution(11939291276794999214)
XLA Ops:
  0.0 44.9 %shard_map.55.f_ref = bf16[320,512]{1,0:T(8,128)(2,1)} custom-call(s32[64,128]{1,0:T(8,128)} %bitcast.1, f32[5,8192]{1,0:T(8,128)} %amp_ref.3, bf16[5,512,128]{2,1,0:T(8,128)(2,1)} %table_any.1, bf16[64,8192]{1,0:T(8,128)(2,1)} %fields_any.1, f32[5,128]{1,0:T(8,128)} %prior_ref.1), custom_call_target="tpu_custom_call" | custom-call | tf_op jit(solution)/shard_map/pallas_call | solution.py:412
  44.9 5.7 %shard_map.56 = f32[64,8192]{1,0:T(8,128)} custom-call(s32[64,128]{1,0:T(8,128)} %bitcast.2, f32[5,8192]{1,0:T(8,128)} %amp_ref.3, bf16[320,512]{1,0:T(8,128)(2,1)} %shard_map.55.f_ref), custom_call_target="tpu_custom_call" | custom-call | tf_op jit(solution)/shard_map/pallas_call | solution.py:438

commit v8 on v7

--- a/solution.py
+++ b/solution.py
@@ -239,7 +239,7 @@
     w_copies = [send(wall_ref.at[obs], wall_ref.at[obs], k, dev) for k, dev in enumerate(y_peers)]
     for load in loads:
         load.wait()
-    accumulate(pattern_ref, acc_ref, n_here, 2048, field_rows)
+    accumulate(pattern_ref, acc_ref, n_here, 4096, field_rows)
     for t in range(tiers):
         v = split2(acc_ref[t * nf:(t + 1) * nf, :])
         both = jnp.dot(v, table_ref[t], preferred_element_type=f32)
@@ -434,7 +434,7 @@
         ],
         compiler_params=pltpu.CompilerParams(collective_id=0, has_side_effects=True),
     )(pattern2, amplitude, basis_table, fields, prior_precision)
-    chunk = min(2048, obs)
+    chunk = min(4096, obs)
     return pl.pallas_call(
         fit_kernel,
         grid=(obs // chunk,),

time: 51 us -> 50.5 us (level)
  no operation moved by 1% of the time
where the time goes in v8:
time: 50.5 us; the launch traced here: 50.2 us
  Pallas kernels  50.2 us (99%)
    pallas_call x1, Pallas kernels, shards(): pl.pallas_call(tree_kernel, out_shape=jax.ShapeDtypeStruct((tiers * nf, p...  44.5 us
    pallas_call x1, Pallas kernels, shards(): pl.pallas_call(fit_kernel, grid=(obs // chunk,), in_specs=[pl.BlockSpec((...  5.7 us

profile of v8, /device:TPU:0, one launch (start us, length us, event | category | flops | bytes accessed | tf_op | source)
XLA Modules:
  0.0 50.2 jit_solution(76481868034392769)
XLA Ops:
  0.0 44.5 %shard_map.55.f_ref = bf16[320,512]{1,0:T(8,128)(2,1)} custom-call(s32[64,128]{1,0:T(8,128)} %bitcast.1, f32[5,8192]{1,0:T(8,128)} %amp_ref.3, bf16[5,512,128]{2,1,0:T(8,128)(2,1)} %table_any.1, bf16[64,8192]{1,0:T(8,128)(2,1)} %fields_any.1, f32[5,128]{1,0:T(8,128)} %prior_ref.1), custom_call_target="tpu_custom_call" | custom-call | tf_op jit(solution)/shard_map/pallas_call | solution.py:412
  44.5 5.7 %shard_map.56 = f32[64,8192]{1,0:T(8,128)} custom-call(s32[64,128]{1,0:T(8,128)} %bitcast.2, f32[5,8192]{1,0:T(8,128)} %amp_ref.3, bf16[320,512]{1,0:T(8,128)(2,1)} %shard_map.55.f_ref), custom_call_target="tpu_custom_call" | custom-call | tf_op jit(solution)/shard_map/pallas_call | solution.py:438
